TPU v7x, 256 devices: a whole 4x4x8 slice. The times are simulated.
256 devices in a mesh: gx: 32 (over y, x, core), gy: 8 (over z).
Axes of the slice: x: 4, y: 4, z: 8, core: 2. Of those that a mesh axis runs over, the one named last changes fastest.
Arguments:
- value_field: float32 [128, 64, 8, 1024], P('gx', 'gy'), may hold values from -6 to 6
- obstacle: float32 [128, 64, 8, 1024], P('gx', 'gy'), may hold values from -4 to 4
- drift_field: float32 [128, 64, 2], P('gx', 'gy'), may hold values from -9 to 9
Outputs:
- value_next: float32 [128, 64, 8, 1024], P('gx', 'gy')
- steps_taken: float32 [4], replicated
All inputs are finite; a program needn't handle non-finite values.
Results may differ from a plain program's by a relative error of at most 0.00002.
Values sent between devices are 32-bit elements; how exact they have to be, the bound alone decides.
A program may use at most 128 MiB of HBM per device.

v0:
```python
import math

import jax
import jax.numpy as jnp
from jax import lax
from jax.sharding import Mesh
from jax.sharding import PartitionSpec as P

NTH = 8
NV = 16
NW = 64
ITERS = 4
GX = ("gx_0", "gx_1", "gx_2")


SPACE_STEP = 0.5
SPEED_BASE = 1.0
SPEED_STEP = 0.2
TURN_LIMIT = 0.25
EFFORT_COST = 10.0
COURANT = 0.9


def from_everyone(shard, axis):
    copies = jnp.broadcast_to(shard, (lax.axis_size(axis), *shard.shape))
    return lax.all_to_all(copies, axis, split_axis=0, concat_axis=0, tiled=True)


def over_copies(shard, axis):
    return from_everyone(shard, axis).max(axis=0)


def one_axis_at_a_time(shard, axes):
    far, near = axes
    nearer = over_copies(shard, near)
    return over_copies(nearer, far)


def packed_total(arrays, axis):
    line, at, gathered = (jnp.concatenate([a.reshape(-1) for a in arrays]), 0, [])
    running = one_axis_at_a_time(line, axis)
    for a in arrays:
        gathered.append(running[at : at + a.size].reshape(a.shape))
        at += a.size
    return tuple(gathered)


def extended_2(shard, sides, width):
    edges = {}
    for axis, dim in sides:
        peers, length = (lax.axis_size(axis), shard.shape[dim])
        up = [(i, (i + 1) % peers) for i in range(peers - 1)]
        last = lax.slice_in_dim(shard, length - width, length, axis=dim)
        first = lax.slice_in_dim(shard, 0, width, axis=dim)
        edges[dim] = (
            lax.ppermute(last, axis, up),
            lax.ppermute(first, axis, [(b, a) for a, b in up]),
        )
    done = []
    for _, dim in sides:
        low, high = edges[dim]
        around = [(width, width) if d in done else (0, 0) for d in range(shard.ndim)]
        shard = jnp.concatenate([jnp.pad(low, around), shard, jnp.pad(high, around)], axis=dim)
        done.append(dim)
    return shard


def grid_lanes():
    heading = jnp.arange(NTH, dtype=jnp.int32).astype(jnp.float32) * (2.0 * math.pi / NTH)
    lane_index = jnp.arange(NV * NW, dtype=jnp.int32)
    speed_row = SPEED_BASE + (lane_index // NW).astype(jnp.float32) * SPEED_STEP
    turning = -1.0 + ((lane_index % NW).astype(jnp.float32) + 0.5) * (2.0 / NW)
    cosine_speed = jnp.cos(heading)[:, None] * speed_row[None, :]
    sine_speed = jnp.sin(heading)[:, None] * speed_row[None, :]
    return (cosine_speed, sine_speed, turning)


def rate_field(drift_part):
    cosine_speed, sine_speed, turning = grid_lanes()
    east_rate = cosine_speed + drift_part[:, :, 0][:, :, None, None]
    north_rate = sine_speed + drift_part[:, :, 1][:, :, None, None]
    head_step = 2.0 * math.pi / NTH
    turn_step = 2.0 / NW
    return (
        jnp.abs(east_rate) / SPACE_STEP
        + jnp.abs(north_rate) / SPACE_STEP
        + jnp.abs(turning) / head_step
        + TURN_LIMIT / turn_step
    )


def advance(extended, drift_part, barrier, time_step, slope_rate):
    center = extended[1:-1, 1:-1]
    east_plus = (extended[2:, 1:-1] - center) / SPACE_STEP
    east_minus = (center - extended[:-2, 1:-1]) / SPACE_STEP
    north_plus = (extended[1:-1, 2:] - center) / SPACE_STEP
    north_minus = (center - extended[1:-1, :-2]) / SPACE_STEP
    head_step = 2.0 * math.pi / NTH
    turn_step = 2.0 / NW
    head_plus = (jnp.roll(center, -1, axis=2) - center) / head_step
    head_minus = (center - jnp.roll(center, 1, axis=2)) / head_step
    speed_diff = (center[..., NW:] - center[..., :-NW]) / SPEED_STEP
    speed_plus = jnp.concatenate([speed_diff, speed_diff[..., -NW:]], axis=3)
    speed_minus = jnp.concatenate([speed_diff[..., :NW], speed_diff], axis=3)
    turn_diff = (center[..., 1:] - center[..., :-1]) / turn_step
    padding = jnp.zeros_like(turn_diff[..., :1])
    forward = jnp.concatenate([turn_diff, padding], axis=3)
    backward = jnp.concatenate([padding, turn_diff], axis=3)
    lane_pos = jnp.arange(center.shape[3], dtype=jnp.int32) % NW
    turn_plus = jnp.where(lane_pos == NW - 1, backward, forward)
    turn_minus = jnp.where(lane_pos == 0, forward, backward)
    cosine_speed, sine_speed, turning = grid_lanes()
    east_rate = cosine_speed + drift_part[:, :, 0][:, :, None, None]
    north_rate = sine_speed + drift_part[:, :, 1][:, :, None, None]
    speed_mean = 0.5 * (speed_plus + speed_minus)
    hamiltonian = (
        east_rate * (0.5 * (east_plus + east_minus))
        + north_rate * (0.5 * (north_plus + north_minus))
        + turning * (0.5 * (head_plus + head_minus))
        + speed_mean * speed_mean / (2.0 * EFFORT_COST)
        + TURN_LIMIT * jnp.abs(0.5 * (turn_plus + turn_minus))
    )
    damping = (
        jnp.abs(east_rate) * (0.5 * (east_plus - east_minus))
        + jnp.abs(north_rate) * (0.5 * (north_plus - north_minus))
        + jnp.abs(turning) * (0.5 * (head_plus - head_minus))
        + slope_rate * (0.5 * (speed_plus - speed_minus))
        + TURN_LIMIT * (0.5 * (turn_plus - turn_minus))
    )
    return jnp.minimum(center + time_step * (hamiltonian + damping), barrier)


def edge_fill(extended, width, low_x, high_x, low_y, high_y):
    inner_x = extended.shape[0] - 2 * width
    inner_y = extended.shape[1] - 2 * width
    left_rim = jnp.where(low_x, 2.0 * extended[width] - extended[width + 1], extended[width - 1])
    extended = extended.at[width - 1].set(left_rim)
    right_at = width + inner_x
    right_rim = jnp.where(
        high_x, 2.0 * extended[right_at - 1] - extended[right_at - 2], extended[right_at]
    )
    extended = extended.at[right_at].set(right_rim)
    lower_rim = jnp.where(
        low_y, 2.0 * extended[:, width] - extended[:, width + 1], extended[:, width - 1]
    )
    extended = extended.at[:, width - 1].set(lower_rim)
    top_at = width + inner_y
    upper_rim = jnp.where(
        high_y, 2.0 * extended[:, top_at - 1] - extended[:, top_at - 2], extended[:, top_at]
    )
    extended = extended.at[:, top_at].set(upper_rim)
    return extended


def per_device(value_field, obstacle, drift_field):
    low_x = lax.axis_index(GX) == 0
    high_x = lax.axis_index(GX) == lax.axis_size(GX) - 1
    low_y = lax.axis_index("gy") == 0
    high_y = lax.axis_index("gy") == lax.axis_size("gy") - 1
    rate_cells = rate_field(drift_field)
    rate_top = None
    step_list = []
    current_value = value_field
    for step_index in range(ITERS):
        extended = extended_2(current_value, ((GX, 0), ("gy", 1)), 1)
        step_rate_top = rate_top
        local_slope = jnp.max(jnp.abs(current_value[..., NW:] - current_value[..., :-NW]))
        if step_index == 0:
            slope_peak, step_rate_top = packed_total(
                (local_slope, jnp.max(rate_cells)), (("gx_0", "gx_1"), ("gx_2", "gy"))
            )
        else:
            slope_peak = one_axis_at_a_time(local_slope, (("gx_0", "gx_1"), ("gx_2", "gy")))
        top_slope = slope_peak / SPEED_STEP
        rate_bound = step_rate_top + top_slope / (EFFORT_COST * SPEED_STEP)
        time_step = COURANT / rate_bound
        slope_rate = top_slope / EFFORT_COST
        rate_top = step_rate_top
        step_list.append(time_step)
        current_value = advance(
            edge_fill(extended, 1, low_x, high_x, low_y, high_y),
            drift_field,
            obstacle,
            time_step,
            slope_rate,
        )
    return (current_value, jnp.stack(step_list))


def solution(mesh):
    finer = Mesh(mesh.devices.reshape(4, 4, 2, mesh.shape["gy"]), ("gx_0", "gx_1", "gx_2", "gy"))
    placed = (P(GX, "gy", None, None), P(GX, "gy", None, None), P(GX, "gy", None))
    return jax.shard_map(
        per_device,
        mesh=finer,
        in_specs=placed,
        out_specs=(P(GX, "gy", None, None), P()),
        check_vma=False,
    )
```

profile of v0, /device:TPU:1, one launch (start us, length us, event | category | flops | bytes accessed | tf_op | source)
XLA Modules:
  0.0 192.7 jit_solution(2082145086420402022)
XLA Ops:
  0.7 2.6 %abs_reduce_fusion = f32[]{:T(128)} fusion(f32[4,8,8,1024]{3,2,1,0:T(8,128)} %param.35), kind=kLoop, calls=%fused_computation.165 | loop fusion | flops 737279 | bytes 1966084 | tf_op jit(solution)/shard_map/reduce_max | solution.py:167
  3.4 1.0 fusion.53
  4.3 1.4 pad_maximum_fusion.8
  5.7 0.6 broadcast_in_dim.41
  6.3 10.0 %all-to-all-start = ((f32[16,1,2]{2,1,0:T(1,128)}), f32[16,1,2]{2,1,0:T(1,128)S(1)}, u32[]{:S(2)}, u32[]{:S(2)}) async-start(f32[16,1,2]{2,1,0:T(1,128)} %broadcast_in_dim.41), calls=%async_computation | async-start | bytes 16384 | tf_op jit(solution)/shard_map/all_to_all | solution.py:26
  16.4 3.1 %collective-permute-start.1 = (f32[1,8,8,1024]{3,2,1,0:T(8,128)S(1)}, f32[1,8,8,1024]{3,2,1,0:T(8,128)S(1)}, u32[]{:S(2)}, u32[]{:S(2)}) collective-permute-start(f32[1,8,8,1024]{3,2,1,0:T(8,128)S(1)} %get-tuple-element.230), channel_id=1, source_target_pairs={{0,8},{8,16},{16,24},{24,32},{32,40},{40,48},{48,56},{56,64},{64,7... | collective-permute-start | bytes 786440 | tf_op jit(solution)/shard_map/ppermute | solution.py:56
  19.5 1.9 collective-permute-start.2
  21.4 3.6 %collective-permute-start = (f32[4,1,8,1024]{3,2,1,0:T(8,128)S(1)}, f32[4,1,8,1024]{3,2,1,0:T(8,128)S(1)}, u32[]{:S(2)}, u32[]{:S(2)}) collective-permute-start(f32[4,1,8,1024]{3,2,1,0:T(8,128)S(1)} %get-tuple-element.232), channel_id=1, source_target_pairs={{0,1},{1,2},{2,3},{3,4},{4,5},{5,6},{6,7},{8,9},{9,10},{10,11},{11... | collective-permute-start | bytes 393224 | tf_op jit(solution)/shard_map/ppermute | solution.py:56
  25.0 1.3 collective-permute-start.3
  26.4 0.6 broadcast_in_dim.42
  27.0 6.5 %all-to-all-start.1 = ((f32[16,1,2]{2,1,0:T(1,128)}), f32[16,1,2]{2,1,0:T(1,128)S(1)}, u32[]{:S(2)}, u32[]{:S(2)}) async-start(f32[16,1,2]{2,1,0:T(1,128)} %broadcast_in_dim.42), calls=%async_computation.1 | async-start | bytes 16384 | tf_op jit(solution)/shard_map/all_to_all | solution.py:26
  33.4 6.3 %all-to-all-done.1 = f32[16,1,2]{2,1,0:T(1,128)S(1)} async-done(((f32[16,1,2]{2,1,0:T(1,128)}), f32[16,1,2]{2,1,0:T(1,128)S(1)}, u32[]{:S(2)}, u32[]{:S(2)}) %all-to-all-start.1) | async-done | bytes 160 | tf_op jit(solution)/shard_map/all_to_all | solution.py:26
  39.8 0.6 fusion.167
  43.2 0.4 fusion.95
  43.6 0.4 fusion.94
  44.3 0.9 copy-done
  45.2 2.7 %fusion.25 = f32[4,8,8,1024]{3,2,1,0:T(8,128)S(1)} fusion(f32[4,8,8,1024]{3,2,1,0:T(8,128)S(1)} %copy-done, f32[4,8,8,1023]{3,2,1,0:T(8,128)S(1)} %fusion.94, f32[4,8,8,960]{3,2,1,0:T(8,128)S(1)} %fusion.95, f32[4,8,8,64]{3,2,1,0:T(8,128)S(1)} %get-tuple-element.229, f32[4,8,8,64]{3,2,1,0:T(8,128)S(1)} %get-tuple-element.228, ...), kind=kLoop, calls=%fused_computation.39 | loop fusion | flops 16252928 | bytes 11674888 | tf_op jit(solution)/shard_map/min | solution.py:130
  48.0 4.7 %collective-permute-start.5 = (f32[1,8,8,1024]{3,2,1,0:T(8,128)S(1)}, f32[1,8,8,1024]{3,2,1,0:T(8,128)S(1)}, u32[]{:S(2)}, u32[]{:S(2)}) collective-permute-start(f32[1,8,8,1024]{3,2,1,0:T(8,128)S(1)} %get-tuple-element.224), channel_id=1, source_target_pairs={{0,8},{8,16},{16,24},{24,32},{32,40},{40,48},{48,56},{56,64},{64,7... | collective-permute-start | bytes 786440 | tf_op jit(solution)/shard_map/ppermute | solution.py:56
  52.7 1.9 collective-permute-start.6
  54.7 4.9 %collective-permute-start.4 = (f32[4,1,8,1024]{3,2,1,0:T(8,128)S(1)}, f32[4,1,8,1024]{3,2,1,0:T(8,128)}, u32[]{:S(2)}, u32[]{:S(2)}) collective-permute-start(f32[4,1,8,1024]{3,2,1,0:T(8,128)S(1)} %get-tuple-element.226), channel_id=1, source_target_pairs={{0,1},{1,2},{2,3},{3,4},{4,5},{5,6},{6,7},{8,9},{9,10},{10,11},{11... | collective-permute-start | bytes 393224 | tf_op jit(solution)/shard_map/ppermute | solution.py:56
  59.6 1.3 collective-permute-start.7
  60.9 1.0 fusion.93
  61.8 0.6 broadcast_in_dim.45
  62.5 16.2 %all_to_all.48 = f32[16,1,1]{2,1,0:T(1,128)S(1)} all-to-all(f32[16,1,1]{2,1,0:T(1,128)S(1)} %broadcast_in_dim.45), channel_id=1, replica_groups=mesh['gx_0'=4,'gx_1'=4,'gx_2'=2,'gy'=8] {'gx_2','gy'}, dimensions={0} | all-to-all | bytes 128 | tf_op jit(solution)/shard_map/all_to_all | solution.py:26
  78.7 0.6 reduce_max.122
  79.3 0.6 broadcast_in_dim.46
  80.0 12.6 %all_to_all.49 = f32[16,1,1]{2,1,0:T(1,128)S(1)} all-to-all(f32[16,1,1]{2,1,0:T(1,128)S(1)} %broadcast_in_dim.46), channel_id=1, replica_groups=mesh['gx_0'=4,'gx_1'=4,'gx_2'=2,'gy'=8] {'gx_0','gx_1'}, dimensions={0} | all-to-all | bytes 128 | tf_op jit(solution)/shard_map/all_to_all | solution.py:26
  92.6 0.6 reduce_max.123
  95.2 1.2 fusion.15
  97.0 0.4 fusion.87
  97.4 0.4 fusion.86
  97.7 0.3 fusion.150
  98.0 2.8 %fusion.33 = f32[4,8,8,1024]{3,2,1,0:T(8,128)S(1)} fusion(f32[4,8,8,1024]{3,2,1,0:T(8,128)S(1)} %copy-done, f32[4,8,8,1023]{3,2,1,0:T(8,128)S(1)} %fusion.86, f32[4,8,8,960]{3,2,1,0:T(8,128)S(1)} %fusion.87, f32[4,8,8,64]{3,2,1,0:T(8,128)S(1)} %get-tuple-element.223, f32[4,8,8,64]{3,2,1,0:T(8,128)S(1)} %get-tuple-element.222, ...), kind=kLoop, calls=%fused_computation.47 | loop fusion | flops 16252928 | bytes 11674888 | tf_op jit(solution)/shard_map/min | solution.py:130
  100.9 4.2 %collective-permute-start.9 = (f32[1,8,8,1024]{3,2,1,0:T(8,128)S(1)}, f32[1,8,8,1024]{3,2,1,0:T(8,128)S(1)}, u32[]{:S(2)}, u32[]{:S(2)}) collective-permute-start(f32[1,8,8,1024]{3,2,1,0:T(8,128)S(1)} %get-tuple-element.218), channel_id=1, source_target_pairs={{0,8},{8,16},{16,24},{24,32},{32,40},{40,48},{48,56},{56,64},{64,7... | collective-permute-start | bytes 786440 | tf_op jit(solution)/shard_map/ppermute | solution.py:56
  105.1 1.9 collective-permute-start.10
  107.1 2.9 %collective-permute-start.8 = (f32[4,1,8,1024]{3,2,1,0:T(8,128)S(1)}, f32[4,1,8,1024]{3,2,1,0:T(8,128)}, u32[]{:S(2)}, u32[]{:S(2)}) collective-permute-start(f32[4,1,8,1024]{3,2,1,0:T(8,128)S(1)} %get-tuple-element.220), channel_id=1, source_target_pairs={{0,1},{1,2},{2,3},{3,4},{4,5},{5,6},{6,7},{8,9},{9,10},{10,11},{11... | collective-permute-start | bytes 393224 | tf_op jit(solution)/shard_map/ppermute | solution.py:56
  109.9 1.3 collective-permute-start.11
  111.2 1.0 fusion.85
  112.2 0.6 broadcast_in_dim.47
  112.9 11.1 %all_to_all.50 = f32[16,1,1]{2,1,0:T(1,128)S(1)} all-to-all(f32[16,1,1]{2,1,0:T(1,128)S(1)} %broadcast_in_dim.47), channel_id=1, replica_groups=mesh['gx_0'=4,'gx_1'=4,'gx_2'=2,'gy'=8] {'gx_2','gy'}, dimensions={0} | all-to-all | bytes 128 | tf_op jit(solution)/shard_map/all_to_all | solution.py:26
  124.0 0.6 reduce_max.125
  124.6 0.6 broadcast_in_dim.48
  125.2 12.6 %all_to_all.51 = f32[16,1,1]{2,1,0:T(1,128)S(1)} all-to-all(f32[16,1,1]{2,1,0:T(1,128)S(1)} %broadcast_in_dim.48), channel_id=1, replica_groups=mesh['gx_0'=4,'gx_1'=4,'gx_2'=2,'gy'=8] {'gx_0','gx_1'}, dimensions={0} | all-to-all | bytes 128 | tf_op jit(solution)/shard_map/all_to_all | solution.py:26
  137.8 0.6 reduce_max.126
  140.5 1.2 fusion.13
  142.3 0.4 fusion.79
  142.6 0.4 fusion.78
  143.3 2.8 %fusion.41 = f32[4,8,8,1024]{3,2,1,0:T(8,128)S(1)} fusion(f32[4,8,8,1024]{3,2,1,0:T(8,128)S(1)} %copy-done, f32[4,8,8,1023]{3,2,1,0:T(8,128)S(1)} %fusion.78, f32[4,8,8,960]{3,2,1,0:T(8,128)S(1)} %fusion.79, f32[4,8,8,64]{3,2,1,0:T(8,128)S(1)} %get-tuple-element.217, f32[4,8,8,64]{3,2,1,0:T(8,128)S(1)} %get-tuple-element.216, ...), kind=kLoop, calls=%fused_computation.55 | loop fusion | flops 16252928 | bytes 11674888 | tf_op jit(solution)/shard_map/min | solution.py:130
  146.2 2.9 %collective-permute-start.12 = (f32[4,1,8,1024]{3,2,1,0:T(8,128)S(1)}, f32[4,1,8,1024]{3,2,1,0:T(8,128)}, u32[]{:S(2)}, u32[]{:S(2)}) collective-permute-start(f32[4,1,8,1024]{3,2,1,0:T(8,128)S(1)} %get-tuple-element.214), channel_id=1, source_target_pairs={{0,1},{1,2},{2,3},{3,4},{4,5},{5,6},{6,7},{8,9},{9,10},{10,11},{11... | collective-permute-start | bytes 393224 | tf_op jit(solution)/shard_map/ppermute | solution.py:56
  149.0 1.3 collective-permute-start.15
  150.3 4.5 %collective-permute-start.13 = (f32[1,8,8,1024]{3,2,1,0:T(8,128)S(1)}, f32[1,8,8,1024]{3,2,1,0:T(8,128)S(1)}, u32[]{:S(2)}, u32[]{:S(2)}) collective-permute-start(f32[1,8,8,1024]{3,2,1,0:T(8,128)S(1)} %get-tuple-element.212), channel_id=1, source_target_pairs={{0,8},{8,16},{16,24},{24,32},{32,40},{40,48},{48,56},{56,64},{64,7... | collective-permute-start | bytes 786440 | tf_op jit(solution)/shard_map/ppermute | solution.py:56
  154.8 1.9 collective-permute-start.14
  156.8 1.0 fusion.77
  157.7 0.6 broadcast_in_dim.96
  158.4 11.4 %all_to_all.52 = f32[16,1,1]{2,1,0:T(1,128)S(1)} all-to-all(f32[16,1,1]{2,1,0:T(1,128)S(1)} %broadcast_in_dim.96), channel_id=1, replica_groups=mesh['gx_0'=4,'gx_1'=4,'gx_2'=2,'gy'=8] {'gx_2','gy'}, dimensions={0} | all-to-all | bytes 128 | tf_op jit(solution)/shard_map/all_to_all | solution.py:26
  169.8 0.6 reduce_max.128
  170.4 0.6 broadcast_in_dim.97
  171.1 12.0 %all_to_all.53 = f32[16,1,1]{2,1,0:T(1,128)S(1)} all-to-all(f32[16,1,1]{2,1,0:T(1,128)S(1)} %broadcast_in_dim.97), channel_id=1, replica_groups=mesh['gx_0'=4,'gx_1'=4,'gx_2'=2,'gy'=8] {'gx_0','gx_1'}, dimensions={0} | all-to-all | bytes 128 | tf_op jit(solution)/shard_map/all_to_all | solution.py:26
  183.1 0.6 reduce_max.129
  185.7 0.6 pad_maximum_fusion.9
  186.3 1.2 select_maximum_fusion
  188.1 0.4 fusion.71
  188.5 0.4 fusion.70
  189.1 3.6 %fusion.49 = f32[4,8,8,1024]{3,2,1,0:T(8,128)} fusion(f32[4,8,8,1024]{3,2,1,0:T(8,128)S(1)} %copy-done, f32[4,8,8,1023]{3,2,1,0:T(8,128)S(1)} %fusion.70, f32[4,8,8,960]{3,2,1,0:T(8,128)S(1)} %fusion.71, f32[4,8,8,64]{3,2,1,0:T(8,128)S(1)} %get-tuple-element.211, f32[4,8,8,64]{3,2,1,0:T(8,128)S(1)} %get-tuple-element.210, ...), kind=kLoop, calls=%fused_computation.63 | loop fusion | flops 16252928 | bytes 11674888 | tf_op jit(solution)/shard_map/min | solution.py:130
  (82 shorter events, 3.8 us)
Async XLA Ops:
  0.6 15.7 %copy-start.1 = (f32[4,8,8,1024]{3,2,1,0:T(8,128)S(1)}, f32[4,8,8,1024]{3,2,1,0:T(8,128)}, u32[]{:S(2)}) copy-start(f32[4,8,8,1024]{3,2,1,0:T(8,128)} %param.35) | copy-start | bytes 3145732
  0.6 2.6 %copy-start.2 = (f32[4,8,2]{1,2,0:T(2,128)S(1)}, f32[4,8,2]{1,2,0:T(2,128)}, u32[]{:S(2)}) copy-start(f32[4,8,2]{1,2,0:T(2,128)} %param.37) | copy-start | bytes 772
  6.3 20.0 %all-to-all-start = ((f32[16,1,2]{2,1,0:T(1,128)}), f32[16,1,2]{2,1,0:T(1,128)S(1)}, u32[]{:S(2)}, u32[]{:S(2)}) async-start(f32[16,1,2]{2,1,0:T(1,128)} %broadcast_in_dim.41), calls=%async_computation | async-start | bytes 16384 | tf_op jit(solution)/shard_map/all_to_all | solution.py:26
  16.4 26.0 %collective-permute-start.1 = (f32[1,8,8,1024]{3,2,1,0:T(8,128)S(1)}, f32[1,8,8,1024]{3,2,1,0:T(8,128)S(1)}, u32[]{:S(2)}, u32[]{:S(2)}) collective-permute-start(f32[1,8,8,1024]{3,2,1,0:T(8,128)S(1)} %get-tuple-element.230), channel_id=1, source_target_pairs={{0,8},{8,16},{16,24},{24,32},{32,40},{40,48},{48,56},{56,64},{64,7... | collective-permute-start | bytes 786440 | tf_op jit(solution)/shard_map/ppermute | solution.py:56
  19.5 22.9 %collective-permute-start.2 = (f32[1,8,8,1024]{3,2,1,0:T(8,128)S(1)}, f32[1,8,8,1024]{3,2,1,0:T(8,128)S(1)}, u32[]{:S(2)}, u32[]{:S(2)}) collective-permute-start(f32[1,8,8,1024]{3,2,1,0:T(8,128)S(1)} %get-tuple-element.231), channel_id=1, source_target_pairs={{8,0},{16,8},{24,16},{32,24},{40,32},{48,40},{56,48},{64,56},{72,6... | collective-permute-start | bytes 786440 | tf_op jit(solution)/shard_map/ppermute | solution.py:57
  21.4 21.0 %collective-permute-start = (f32[4,1,8,1024]{3,2,1,0:T(8,128)S(1)}, f32[4,1,8,1024]{3,2,1,0:T(8,128)S(1)}, u32[]{:S(2)}, u32[]{:S(2)}) collective-permute-start(f32[4,1,8,1024]{3,2,1,0:T(8,128)S(1)} %get-tuple-element.232), channel_id=1, source_target_pairs={{0,1},{1,2},{2,3},{3,4},{4,5},{5,6},{6,7},{8,9},{9,10},{10,11},{11... | collective-permute-start | bytes 393224 | tf_op jit(solution)/shard_map/ppermute | solution.py:56
  25.0 17.4 %collective-permute-start.3 = (f32[4,1,8,1024]{3,2,1,0:T(8,128)S(1)}, f32[4,1,8,1024]{3,2,1,0:T(8,128)S(1)}, u32[]{:S(2)}, u32[]{:S(2)}) collective-permute-start(f32[4,1,8,1024]{3,2,1,0:T(8,128)S(1)} %get-tuple-element.233), channel_id=1, source_target_pairs={{1,0},{2,1},{3,2},{4,3},{5,4},{6,5},{7,6},{9,8},{10,9},{11,10},{12... | collective-permute-start | bytes 393224 | tf_op jit(solution)/shard_map/ppermute | solution.py:57
  27.0 12.8 %all-to-all-start.1 = ((f32[16,1,2]{2,1,0:T(1,128)}), f32[16,1,2]{2,1,0:T(1,128)S(1)}, u32[]{:S(2)}, u32[]{:S(2)}) async-start(f32[16,1,2]{2,1,0:T(1,128)} %broadcast_in_dim.42), calls=%async_computation.1 | async-start | bytes 16384 | tf_op jit(solution)/shard_map/all_to_all | solution.py:26
  44.0 1.2 copy-start
  48.0 47.2 %collective-permute-start.5 = (f32[1,8,8,1024]{3,2,1,0:T(8,128)S(1)}, f32[1,8,8,1024]{3,2,1,0:T(8,128)S(1)}, u32[]{:S(2)}, u32[]{:S(2)}) collective-permute-start(f32[1,8,8,1024]{3,2,1,0:T(8,128)S(1)} %get-tuple-element.224), channel_id=1, source_target_pairs={{0,8},{8,16},{16,24},{24,32},{32,40},{40,48},{48,56},{56,64},{64,7... | collective-permute-start | bytes 786440 | tf_op jit(solution)/shard_map/ppermute | solution.py:56
  52.7 42.5 %collective-permute-start.6 = (f32[1,8,8,1024]{3,2,1,0:T(8,128)S(1)}, f32[1,8,8,1024]{3,2,1,0:T(8,128)S(1)}, u32[]{:S(2)}, u32[]{:S(2)}) collective-permute-start(f32[1,8,8,1024]{3,2,1,0:T(8,128)S(1)} %get-tuple-element.225), channel_id=1, source_target_pairs={{8,0},{16,8},{24,16},{32,24},{40,32},{48,40},{56,48},{64,56},{72,6... | collective-permute-start | bytes 786440 | tf_op jit(solution)/shard_map/ppermute | solution.py:57
  54.7 40.5 %collective-permute-start.4 = (f32[4,1,8,1024]{3,2,1,0:T(8,128)S(1)}, f32[4,1,8,1024]{3,2,1,0:T(8,128)}, u32[]{:S(2)}, u32[]{:S(2)}) collective-permute-start(f32[4,1,8,1024]{3,2,1,0:T(8,128)S(1)} %get-tuple-element.226), channel_id=1, source_target_pairs={{0,1},{1,2},{2,3},{3,4},{4,5},{5,6},{6,7},{8,9},{9,10},{10,11},{11... | collective-permute-start | bytes 393224 | tf_op jit(solution)/shard_map/ppermute | solution.py:56
  59.6 35.6 %collective-permute-start.7 = (f32[4,1,8,1024]{3,2,1,0:T(8,128)S(1)}, f32[4,1,8,1024]{3,2,1,0:T(8,128)}, u32[]{:S(2)}, u32[]{:S(2)}) collective-permute-start(f32[4,1,8,1024]{3,2,1,0:T(8,128)S(1)} %get-tuple-element.227), channel_id=1, source_target_pairs={{1,0},{2,1},{3,2},{4,3},{5,4},{6,5},{7,6},{9,8},{10,9},{11,10},{12... | collective-permute-start | bytes 393224 | tf_op jit(solution)/shard_map/ppermute | solution.py:57
  100.9 39.6 %collective-permute-start.9 = (f32[1,8,8,1024]{3,2,1,0:T(8,128)S(1)}, f32[1,8,8,1024]{3,2,1,0:T(8,128)S(1)}, u32[]{:S(2)}, u32[]{:S(2)}) collective-permute-start(f32[1,8,8,1024]{3,2,1,0:T(8,128)S(1)} %get-tuple-element.218), channel_id=1, source_target_pairs={{0,8},{8,16},{16,24},{24,32},{32,40},{40,48},{48,56},{56,64},{64,7... | collective-permute-start | bytes 786440 | tf_op jit(solution)/shard_map/ppermute | solution.py:56
  105.1 35.4 %collective-permute-start.10 = (f32[1,8,8,1024]{3,2,1,0:T(8,128)S(1)}, f32[1,8,8,1024]{3,2,1,0:T(8,128)S(1)}, u32[]{:S(2)}, u32[]{:S(2)}) collective-permute-start(f32[1,8,8,1024]{3,2,1,0:T(8,128)S(1)} %get-tuple-element.219), channel_id=1, source_target_pairs={{8,0},{16,8},{24,16},{32,24},{40,32},{48,40},{56,48},{64,56},{72,6... | collective-permute-start | bytes 786440 | tf_op jit(solution)/shard_map/ppermute | solution.py:57
  107.1 33.4 %collective-permute-start.8 = (f32[4,1,8,1024]{3,2,1,0:T(8,128)S(1)}, f32[4,1,8,1024]{3,2,1,0:T(8,128)}, u32[]{:S(2)}, u32[]{:S(2)}) collective-permute-start(f32[4,1,8,1024]{3,2,1,0:T(8,128)S(1)} %get-tuple-element.220), channel_id=1, source_target_pairs={{0,1},{1,2},{2,3},{3,4},{4,5},{5,6},{6,7},{8,9},{9,10},{10,11},{11... | collective-permute-start | bytes 393224 | tf_op jit(solution)/shard_map/ppermute | solution.py:56
  109.9 30.5 %collective-permute-start.11 = (f32[4,1,8,1024]{3,2,1,0:T(8,128)S(1)}, f32[4,1,8,1024]{3,2,1,0:T(8,128)}, u32[]{:S(2)}, u32[]{:S(2)}) collective-permute-start(f32[4,1,8,1024]{3,2,1,0:T(8,128)S(1)} %get-tuple-element.221), channel_id=1, source_target_pairs={{1,0},{2,1},{3,2},{4,3},{5,4},{6,5},{7,6},{9,8},{10,9},{11,10},{12... | collective-permute-start | bytes 393224 | tf_op jit(solution)/shard_map/ppermute | solution.py:57
  146.2 40.1 %collective-permute-start.12 = (f32[4,1,8,1024]{3,2,1,0:T(8,128)S(1)}, f32[4,1,8,1024]{3,2,1,0:T(8,128)}, u32[]{:S(2)}, u32[]{:S(2)}) collective-permute-start(f32[4,1,8,1024]{3,2,1,0:T(8,128)S(1)} %get-tuple-element.214), channel_id=1, source_target_pairs={{0,1},{1,2},{2,3},{3,4},{4,5},{5,6},{6,7},{8,9},{9,10},{10,11},{11... | collective-permute-start | bytes 393224 | tf_op jit(solution)/shard_map/ppermute | solution.py:56
  149.0 37.3 %collective-permute-start.15 = (f32[4,1,8,1024]{3,2,1,0:T(8,128)S(1)}, f32[4,1,8,1024]{3,2,1,0:T(8,128)}, u32[]{:S(2)}, u32[]{:S(2)}) collective-permute-start(f32[4,1,8,1024]{3,2,1,0:T(8,128)S(1)} %get-tuple-element.215), channel_id=1, source_target_pairs={{1,0},{2,1},{3,2},{4,3},{5,4},{6,5},{7,6},{9,8},{10,9},{11,10},{12... | collective-permute-start | bytes 393224 | tf_op jit(solution)/shard_map/ppermute | solution.py:57
  150.3 36.0 %collective-permute-start.13 = (f32[1,8,8,1024]{3,2,1,0:T(8,128)S(1)}, f32[1,8,8,1024]{3,2,1,0:T(8,128)S(1)}, u32[]{:S(2)}, u32[]{:S(2)}) collective-permute-start(f32[1,8,8,1024]{3,2,1,0:T(8,128)S(1)} %get-tuple-element.212), channel_id=1, source_target_pairs={{0,8},{8,16},{16,24},{24,32},{32,40},{40,48},{48,56},{56,64},{64,7... | collective-permute-start | bytes 786440 | tf_op jit(solution)/shard_map/ppermute | solution.py:56
  154.8 31.5 %collective-permute-start.14 = (f32[1,8,8,1024]{3,2,1,0:T(8,128)S(1)}, f32[1,8,8,1024]{3,2,1,0:T(8,128)S(1)}, u32[]{:S(2)}, u32[]{:S(2)}) collective-permute-start(f32[1,8,8,1024]{3,2,1,0:T(8,128)S(1)} %get-tuple-element.213), channel_id=1, source_target_pairs={{8,0},{16,8},{24,16},{32,24},{40,32},{48,40},{56,48},{64,56},{72,6... | collective-permute-start | bytes 786440 | tf_op jit(solution)/shard_map/ppermute | solution.py:57
where the time goes:
time: 194 us; the launch traced here: 193 us
  blocking collectives  76 us (39%)
  starting transfers between devices  60.1 us (31%)
  other arithmetic  32.3 us (17%)
  between operations  9.4 us (5%)
  local copies, waits for them, and re-layouts  8.64 us (4%)
  waiting for transfers between devices  6.37 us (3%)
    all_to_all x6, blocking collectives, from_everyone(): return lax.all_to_all(copies, axis, split_axis=0, concat_axis=0, tiled=True)  76 us
    ppermute x8, starting transfers between devices, extended_2(): lax.ppermute(last, axis, up)  30.8 us
    all_to_all x2, starting transfers between devices, from_everyone(): return lax.all_to_all(copies, axis, split_axis=0, concat_axis=0, tiled=True)  16.4 us
    ppermute x8, starting transfers between devices, extended_2(): lax.ppermute(first, axis, [(b, a) for a, b in up])  12.8 us
    min x4, other arithmetic, advance(): return jnp.minimum(center + time_step * (hamiltonian + damping), barrier)  11.8 us
    all_to_all x2, waiting for transfers between devices, from_everyone(): return lax.all_to_all(copies, axis, split_axis=0, concat_axis=0, tiled=True)  6.33 us
    reduce_max x4, other arithmetic, per_device(): jnp.max(jnp.abs(current_value[..., NW:] - current_value[..., :-NW]))  5.48 us
    broadcast_in_dim x8, local copies, waits for them, and re-layouts, from_everyone(): copies = jnp.broadcast_to(shard, (lax.axis_size(axis), *shard.shape))  5.08 us
  transfers between devices with their start and end apart: 18, of which 1 were waited for; matrix products, arithmetic and copies ran while one was open for 6% of the time, Pallas kernels for 0%

commit v1 on v0

v1 whole, which is shorter than its diff:
```python
import functools
import math

import jax
import jax.numpy as jnp
import numpy as np
from jax import lax
from jax.experimental import pallas as pl
from jax.experimental.pallas import tpu as pltpu
from jax.sharding import PartitionSpec as P

NTH = 8
NV = 16
NW = 64
ITERS = 4
SPACE_STEP = 0.5
SPEED_BASE = 1.0
SPEED_STEP = 0.2
TURN_LIMIT = 0.25
EFFORT_COST = 10.0
COURANT = 0.9

LANES = 128
GROUPS = NV * NW // LANES
CHIP_X = 4
CHIP_Y = 4
CORES = 2
MESH = pl.DeviceIdType.MESH

HEAD_STEP = 2.0 * math.pi / NTH
TURN_STEP = 2.0 / NW
SCALE = TURN_LIMIT / TURN_STEP


def tables():
    heading = (np.arange(NTH, dtype=np.float32) * np.float32(2.0 * math.pi / NTH)).astype(np.float32)
    lane = np.arange(NV * NW)
    speed = (np.float32(SPEED_BASE) + (lane // NW).astype(np.float32) * np.float32(SPEED_STEP)).astype(np.float32)
    turning = (np.float32(-1.0) + ((lane % NW).astype(np.float32) + np.float32(0.5)) * np.float32(2.0 / NW)).astype(np.float32)
    cosine = np.cos(heading.astype(np.float64)).astype(np.float32)
    sine = np.sin(heading.astype(np.float64)).astype(np.float32)
    factor = np.float32(1.0 / (SPACE_STEP * SCALE))
    east = cosine[:, None] * speed[None, :] * factor
    north = sine[:, None] * speed[None, :] * factor
    turn = np.abs(turning[:LANES]) / np.float32(HEAD_STEP * SCALE)
    turn = np.broadcast_to(turn, (NTH, LANES))
    turn_top = float(np.max(np.abs(turning) / np.float32(HEAD_STEP)))
    return np.stack([east, north]).astype(np.float32), turn.astype(np.float32), turn_top


def kernel(nx, ny, bx, by, turn_top,
           drift, table, turn_table, value_hbm, barrier_hbm, out_hbm, steps_out,
           vb, ob, part_a, part_b, new, sent, got,
           in_sem, ob_sem, out_sem, halo_send, halo_recv, max_send, max_recv):
    me_x = lax.axis_index("gx")
    me_y = lax.axis_index("gy")
    chip = me_x // CORES
    core = me_x % CORES
    chip_y = chip // CHIP_X
    chip_x = chip % CHIP_X
    low_x, high_x = me_x > 0, me_x < nx - 1
    low_y, high_y = me_y > 0, me_y < ny - 1

    column = []
    for k in range(1, CORES * ny):
        other_core = lax.rem(core + k % CORES, CORES)
        other_y = lax.rem(me_y + k // CORES, ny)
        column.append((chip * CORES + other_core, other_y))
    plane = []
    for k in range(1, CHIP_Y * CHIP_X):
        other_cy = lax.rem(chip_y + k // CHIP_X, CHIP_Y)
        other_cx = lax.rem(chip_x + k % CHIP_X, CHIP_X)
        plane.append(((other_cy * CHIP_X + other_cx) * CORES + core, me_y))
    groups = (column, plane)
    sides = ((low_x, (me_x - 1, me_y)), (high_x, (me_x + 1, me_y)),
             (low_y, (me_x, me_y - 1)), (high_y, (me_x, me_y + 1)))

    loads = []
    for i in range(bx):
        copy = pltpu.make_async_copy(value_hbm.at[i], vb.at[0, i + 1, pl.ds(1, by)], in_sem.at[i])
        copy.start()
        loads.append(copy)
    ob_copy = pltpu.make_async_copy(barrier_hbm, ob, ob_sem)
    ob_copy.start()

    ready = pltpu.get_barrier_semaphore()
    for peer in plane + column:
        pl.semaphore_signal(ready, inc=1, device_id=peer, device_id_type=MESH)
    for exists, peer in sides:
        @pl.when(exists)
        def _(peer=peer):
            pl.semaphore_signal(ready, inc=1, device_id=peer, device_id_type=MESH)

    lane = lax.broadcasted_iota(jnp.int32, (NTH, LANES), 1)
    low_half = lane < NW
    in_row = lax.rem(lane, NW)
    first_turn = in_row == 0
    last_turn = in_row == NW - 1
    turn_up = in_row >= NW // 2
    turn_w = turn_table[...]

    def lanes_of(g):
        return slice(g * LANES, (g + 1) * LANES)

    def row_slope(vals, top):
        swapped = [pltpu.roll(v, NW, 1) for v in vals]
        for g in range(GROUPS):
            after = swapped[g + 1] if g + 1 < GROUPS else vals[g]
            ahead = jnp.where(low_half, swapped[g], after)
            top = jnp.maximum(top, jnp.abs(ahead - vals[g]))
        return top

    def one_row(top):
        return jnp.max(top, axis=0, keepdims=True)

    def rate_row(r, top):
        i, j = r // by, lax.rem(r, by)
        dx = drift[i, j * 2] * (1.0 / (SPACE_STEP * SCALE))
        dy = drift[i, j * 2 + 1] * (1.0 / (SPACE_STEP * SCALE))
        for g in range(GROUPS):
            east = table[0, :, lanes_of(g)] + dx
            north = table[1, :, lanes_of(g)] + dy
            top = jnp.maximum(top, jnp.abs(east) + jnp.abs(north))
        return top

    zero = jnp.zeros((NTH, LANES), jnp.float32)
    rate = lax.fori_loop(0, bx * by, rate_row, zero)

    top = zero
    for i in range(bx):
        loads[i].wait()

        def first_slope(j, top, i=i):
            return row_slope([vb[0, i + 1, j + 1, :, lanes_of(g)] for g in range(GROUPS)], top)

        top = lax.fori_loop(0, by, first_slope, top)

    expected = 2 * (len(plane))
    expected = expected + sum(jnp.where(exists, 1, 0) for exists, _ in sides)
    pl.semaphore_wait(ready, expected)

    def spread(step, stage):
        for k, peer in enumerate(groups[stage]):
            pltpu.make_async_remote_copy(
                src_ref=sent.at[step, stage], dst_ref=got.at[step, stage, k],
                send_sem=max_send.at[step, stage], recv_sem=max_recv.at[step, stage],
                device_id=peer, device_id_type=MESH).start()

    def collect(step, stage):
        pltpu.make_async_copy(got.at[step, stage], got.at[step, stage], max_recv.at[step, stage]).wait()
        best = sent[step, stage]
        for k in range(len(groups[stage])):
            best = jnp.maximum(best, got[step, stage, k])
        return best

    def halo_copy(step, side):
        inner = {0: (1, pl.ds(1, by)), 1: (bx, pl.ds(1, by)), 2: (pl.ds(1, bx), 1), 3: (pl.ds(1, bx), by)}[side]
        outer = {0: (bx + 1, pl.ds(1, by)), 1: (0, pl.ds(1, by)), 2: (pl.ds(1, bx), by + 1), 3: (pl.ds(1, bx), 0)}[side]
        return pltpu.make_async_remote_copy(
            src_ref=vb.at[(step,) + inner], dst_ref=vb.at[(step,) + outer],
            send_sem=halo_send.at[step, side], recv_sem=halo_recv.at[step, side],
            device_id=sides[side][1], device_id_type=MESH)

    opposite = (1, 0, 3, 2)

    def ghost(step, side):
        if side < 2:
            to, near, far = ((0, 1, 2), (bx + 1, bx, bx - 1))[side]

            def fill(j, carry):
                vb[step, to, j] = 2.0 * vb[step, near, j] - vb[step, far, j]
                return carry

            lax.fori_loop(1, by + 1, fill, 0)
        else:
            to, near, far = ((0, 1, 2), (by + 1, by, by - 1))[side - 2]

            def fill(i, carry):
                vb[step, i, to] = 2.0 * vb[step, i, near] - vb[step, i, far]
                return carry

            lax.fori_loop(1, bx + 1, fill, 0)

    rate_top = None
    for step in range(ITERS):
        row = one_row(top)
        if step == 0:
            rates = one_row(rate)
            row = jnp.maximum(row, pltpu.roll(row, NW, 1))
            rates = jnp.maximum(rates, pltpu.roll(rates, NW, 1))
            row = jnp.where(low_half[:1], row, rates)
        sent[step, 0] = row
        spread(step, 0)
        for side in range(4):
            @pl.when(sides[side][0])
            def _(side=side):
                halo_copy(step, side).start()

        def inner_terms(r, carry):
            i, j = r // by + 1, lax.rem(r, by) + 1
            vals = [vb[step, i, j, :, lanes_of(g)] for g in range(GROUPS)]
            swapped = [pltpu.roll(v, NW, 1) for v in vals]
            for g in range(GROUPS):
                v = vals[g]
                ahead = jnp.where(low_half, swapped[g], swapped[min(g + 1, GROUPS - 1)]) - v
                behind = jnp.where(low_half, swapped[max(g - 1, 0)], swapped[g]) - v
                if g == 0:
                    behind = jnp.where(low_half, -ahead, behind)
                if g == GROUPS - 1:
                    ahead = jnp.where(low_half, ahead, -behind)
                span = ahead - behind
                part_b[i - 1, j - 1, :, lanes_of(g)] = ahead + behind
                acc = span * span * (1.0 / (4.0 * SPEED_STEP * SPEED_STEP * 2.0 * EFFORT_COST * SCALE))
                right = pltpu.roll(v, LANES - 1, 1) - v
                left = pltpu.roll(v, 1, 1) - v
                acc += jnp.maximum(jnp.where(last_turn, -left, right), jnp.where(first_turn, -right, left))
                around = jnp.where(turn_up, pltpu.roll(v, NTH - 1, 0), pltpu.roll(v, 1, 0))
                acc += turn_w * (around - v)
                part_a[i - 1, j - 1, :, lanes_of(g)] = acc
            return carry

        lax.fori_loop(0, bx * by, inner_terms, 0)

        for side in range(4):
            @pl.when(jnp.logical_not(sides[side][0]))
            def _(side=side):
                ghost(step, side)

        sent[step, 1] = collect(step, 0)
        spread(step, 1)

        for side in range(4):
            @pl.when(sides[side][0])
            def _(side=side):
                rim = vb.at[(step,) + {0: (0, pl.ds(1, by)), 1: (bx + 1, pl.ds(1, by)),
                                       2: (pl.ds(1, bx), 0), 3: (pl.ds(1, bx), by + 1)}[side]]
                pltpu.make_async_copy(rim, rim, halo_recv.at[step, opposite[side]]).wait()

        def position_terms(r, carry):
            i, j = r // by + 1, lax.rem(r, by) + 1
            dx = drift[i - 1, (j - 1) * 2] * (1.0 / (SPACE_STEP * SCALE))
            dy = drift[i - 1, (j - 1) * 2 + 1] * (1.0 / (SPACE_STEP * SCALE))
            for g in range(GROUPS):
                s = lanes_of(g)
                v = vb[step, i, j, :, s]
                east = table[0, :, s] + dx
                north = table[1, :, s] + dy
                from_x = jnp.where(east > 0.0, vb[step, i + 1, j, :, s], vb[step, i - 1, j, :, s])
                from_y = jnp.where(north > 0.0, vb[step, i, j + 1, :, s], vb[step, i, j - 1, :, s])
                part_a[i - 1, j - 1, :, s] += jnp.abs(east) * (from_x - v) + jnp.abs(north) * (from_y - v)
            return carry

        lax.fori_loop(0, bx * by, position_terms, 0)

        best = collect(step, 1)
        if step == 0:
            ob_copy.wait()
            rate_top = jnp.max(jnp.where(low_half[:1], 0.0, best), axis=1, keepdims=True) * SCALE + turn_top + SCALE
            best = jnp.where(low_half[:1], best, 0.0)
        top_slope = jnp.max(best, axis=1, keepdims=True) / SPEED_STEP
        dt = COURANT / (rate_top + top_slope / (EFFORT_COST * SPEED_STEP))
        steps_out[step] = jnp.max(dt)
        weight_a = jnp.broadcast_to(SCALE * dt, (NTH, LANES))
        weight_b = jnp.broadcast_to(dt * (top_slope / EFFORT_COST) * (0.5 / SPEED_STEP), (NTH, LANES))

        def update(r, top):
            i, j = r // by, lax.rem(r, by)
            vals = []
            for g in range(GROUPS):
                s = lanes_of(g)
                moved = (vb[step, i + 1, j + 1, :, s] + weight_a * part_a[i, j, :, s]) + weight_b * part_b[i, j, :, s]
                moved = jnp.minimum(moved, ob[i, j, :, s])
                if step < ITERS - 1:
                    vb[step + 1, i + 1, j + 1, :, s] = moved
                else:
                    new[i, j, :, s] = moved
                vals.append(moved)
            return row_slope(vals, top) if step < ITERS - 1 else top

        if step < ITERS - 1:
            top = lax.fori_loop(0, bx * by, update, zero)
        else:
            stores = []
            for i in range(bx):
                lax.fori_loop(i * by, (i + 1) * by, update, zero)
                copy = pltpu.make_async_copy(new.at[i], out_hbm.at[i], out_sem.at[i])
                copy.start()
                stores.append(copy)

    for step in range(ITERS):
        for stage in range(2):
            pltpu.make_async_copy(got.at[step, stage], got.at[step, stage], max_send.at[step, stage]).wait()
        for side in range(4):
            @pl.when(sides[side][0])
            def _(side=side, step=step):
                halo_copy(step, side).wait_send()
    for copy in stores:
        copy.wait()


def per_device(nx, ny, value_field, obstacle, drift_field):
    bx, by = value_field.shape[:2]
    table, turn_table, turn_top = tables()
    shape = value_field.shape
    peers = CHIP_X * CHIP_Y - 1
    vmem = pl.BlockSpec(memory_space=pltpu.VMEM)
    smem = pl.BlockSpec(memory_space=pltpu.SMEM)
    hbm = pl.BlockSpec(memory_space=pl.ANY)
    dma = pltpu.SemaphoreType.DMA
    return pl.pallas_call(
        functools.partial(kernel, nx, ny, bx, by, turn_top),
        out_shape=(jax.ShapeDtypeStruct(shape, jnp.float32), jax.ShapeDtypeStruct((ITERS,), jnp.float32)),
        in_specs=[smem, vmem, vmem, hbm, hbm],
        out_specs=(hbm, smem),
        scratch_shapes=[
            pltpu.VMEM((ITERS, bx + 2, by + 2) + shape[2:], jnp.float32),
            pltpu.VMEM(shape, jnp.float32),
            pltpu.VMEM(shape, jnp.float32),
            pltpu.VMEM(shape, jnp.float32),
            pltpu.VMEM(shape, jnp.float32),
            pltpu.VMEM((ITERS, 2, 1, LANES), jnp.float32),
            pltpu.VMEM((ITERS, 2, peers, 1, LANES), jnp.float32),
            dma((bx,)), dma, dma((bx,)),
            dma((ITERS, 4)), dma((ITERS, 4)), dma((ITERS, 2)), dma((ITERS, 2)),
        ],
        compiler_params=pltpu.CompilerParams(
            collective_id=0, has_side_effects=True, vmem_limit_bytes=32 * 1024 * 1024),
        name="safe_set_steps",
    )(drift_field.reshape(bx, by * 2), table, turn_table, value_field, obstacle)


def solution(mesh):
    nx, ny = mesh.shape["gx"], mesh.shape["gy"]
    placed = (P("gx", "gy", None, None), P("gx", "gy", None, None), P("gx", "gy", None))
    return jax.shard_map(
        functools.partial(per_device, nx, ny),
        mesh=mesh,
        in_specs=placed,
        out_specs=(P("gx", "gy", None, None), P()),
        check_vma=False,
    )
```

time: 194 us -> 64.5 us (0.33)
  blocking collectives: 76 us -> 0 us
  starting transfers between devices: 60.1 us -> 0 us
  Pallas kernels: 0 us -> 57.4 us
  other arithmetic: 32.3 us -> 0 us
  between operations: 9.4 us -> 0.64 us
  waiting for transfers between devices: 6.37 us -> 0 us
  local copies, waits for them, and re-layouts: 8.64 us -> 6.23 us
    all_to_all x6 -> x0, blocking collectives: 76 us -> none  [from_everyone(): return lax.all_to_all(copies, axis, split_axis=0, concat_axis=0, tiled=True)]
    pallas_call x0 -> x1, Pallas kernels: none -> 57.4 us  [per_device(): pl.pallas_call(functools.partial(kernel, nx, ny, bx, by, turn_top), out_s...]
    ppermute x16 -> x0, starting transfers between devices: 43.6 us -> none  [the longest x8 30.8 us: extended_2(): lax.ppermute(last, axis, up)]
    all_to_all x2 -> x0, starting transfers between devices: 16.4 us -> none  [from_everyone(): return lax.all_to_all(copies, axis, split_axis=0, concat_axis=0, tiled=True)]
    min x4 -> x0, other arithmetic: 11.8 us -> none  [advance(): return jnp.minimum(center + time_step * (hamiltonian + damping), barrier)]
    reduce_max x13 -> x0, other arithmetic: 10.3 us -> none  [the longest x4 5.48 us: per_device(): jnp.max(jnp.abs(current_value[..., NW:] - current_value[..., :-NW]))]
    all_to_all x2 -> x0, waiting for transfers between devices: 6.33 us -> none  [from_everyone(): return lax.all_to_all(copies, axis, split_axis=0, concat_axis=0, tiled=True)]
    unnamed x6 -> x11, local copies, waits for them, and re-layouts: 0.93 us -> 6.15 us
  transfers between devices with their start and end apart: 18 -> 0, of which waited for: 1 -> 0; matrix products, arithmetic and copies ran while one was open for 6% -> 0% of each run, Pallas kernels for 0% -> 0%
where the time goes in v1:
time: 64.5 us; the launch traced here: 64.2 us
  Pallas kernels  57.4 us (89%)
  local copies, waits for them, and re-layouts  6.23 us (10%)
    pallas_call x1, Pallas kernels, per_device(): pl.pallas_call(functools.partial(kernel, nx, ny, bx, by, turn_top), out_s...  57.4 us
    unnamed x11, local copies, waits for them, and re-layouts  6.15 us

profile of v1, /device:TPU:1, one launch (start us, length us, event | category | flops | bytes accessed | tf_op | source)
XLA Modules:
  0.0 64.2 jit_solution(10404059826358752281)
XLA Ops:
  0.6 0.8 %copy.7 = f32[4,8,2]{0,2,1:T(2,128)S(1)} copy(f32[4,8,2]{1,2,0:T(2,128)} %param.7) | data formatting | bytes 512 | tf_op args[2]
  1.4 0.0 copy-start.3
  1.4 0.1 copy.8.drift
  1.5 0.6 copy-done.3
  2.1 0.0 copy-start
  2.1 1.2 %copy-done = f32[4,8,8,1024]{3,2,1,0:T(8,128)S(1)} copy-done((f32[4,8,8,1024]{3,2,1,0:T(8,128)S(1)}, f32[4,8,8,1024]{3,2,1,0:T(8,128)}, u32[]{:S(2)}) %copy-start) | copy-done | bytes 1048600
  3.3 0.0 copy-start.1
  3.3 1.2 %copy-done.1 = f32[4,8,8,1024]{3,2,1,0:T(8,128)S(1)} copy-done((f32[4,8,8,1024]{3,2,1,0:T(8,128)S(1)}, f32[4,8,8,1024]{3,2,1,0:T(8,128)}, u32[]{:S(2)}) %copy-start.1) | copy-done | bytes 1048600
  4.5 0.0 copy-start.2
  4.5 0.8 %copy-done.2 = f32[2,8,1024]{2,1,0:T(8,128)S(1)} copy-done((f32[2,8,1024]{2,1,0:T(8,128)S(1)}, f32[2,8,1024]{2,1,0:T(8,128)}, u32[]{:S(2)}) %copy-start.2) | copy-done | bytes 65560
  5.4 57.4 %safe_set_steps.1 = (f32[4,8,8,1024]{3,2,1,0:T(8,128)S(1)}, f32[4]{0:T(128)S(1)}) custom-call(f32[4,16]{1,0:T(4,128)S(1)} %copy.8.drift, f32[2,8,1024]{2,1,0:T(8,128)S(1)} %copy-done.2, f32[8,128]{1,0:T(8,128)S(1)} %copy-done.3, f32[4,8,8,1024]{3,2,1,0:T(8,128)S(1)} %copy-done, f32[4,8,8,1024]{3,2,1,0:T(8,128)S(1)} %copy-done.1), custom_call_target="tpu_custom_call" | custom-call | tf_op jit(solution)/shard_map/safe_set_steps/pallas_call | solution.py:310
  62.8 1.0 %copy.11 = f32[4,8,8,1024]{3,2,1,0:T(8,128)} copy(f32[4,8,8,1024]{3,2,1,0:T(8,128)S(1)} %get-tuple-element.4) | data formatting | bytes 2097152
  63.7 0.5 copy.12
Async XLA Ops:
  1.4 0.7 %copy-start.3 = (f32[8,128]{1,0:T(8,128)S(1)}, f32[8,128]{1,0:T(8,128)}, u32[]{:S(2)}) copy-start(f32[8,128]{1,0:T(8,128)} %constant.5.clone.turn_table) | copy-start | bytes 12292
  2.1 1.2 %copy-start = (f32[4,8,8,1024]{3,2,1,0:T(8,128)S(1)}, f32[4,8,8,1024]{3,2,1,0:T(8,128)}, u32[]{:S(2)}) copy-start(f32[4,8,8,1024]{3,2,1,0:T(8,128)} %value_hbm.1) | copy-start | bytes 3145732
  3.3 1.2 %copy-start.1 = (f32[4,8,8,1024]{3,2,1,0:T(8,128)S(1)}, f32[4,8,8,1024]{3,2,1,0:T(8,128)}, u32[]{:S(2)}) copy-start(f32[4,8,8,1024]{3,2,1,0:T(8,128)} %barrier_hbm.1) | copy-start | bytes 3145732
  4.5 0.8 %copy-start.2 = (f32[2,8,1024]{2,1,0:T(8,128)S(1)}, f32[2,8,1024]{2,1,0:T(8,128)}, u32[]{:S(2)}) copy-start(f32[2,8,1024]{2,1,0:T(8,128)} %constant.4.clone.table) | copy-start | bytes 196612

commit v2 on v1

v2 whole, which is shorter than its diff:
```python
import functools
import math

import jax
import jax.numpy as jnp
import numpy as np
from jax import lax
from jax.experimental import pallas as pl
from jax.experimental.pallas import tpu as pltpu
from jax.sharding import PartitionSpec as P

NTH = 8
NV = 16
NW = 64
ITERS = 4
SPACE_STEP = 0.5
SPEED_BASE = 1.0
SPEED_STEP = 0.2
TURN_LIMIT = 0.25
EFFORT_COST = 10.0
COURANT = 0.9

LANES = 128
GROUPS = NV * NW // LANES
CHIP_X = 4
CHIP_Y = 4
CORES = 2
MESH = pl.DeviceIdType.MESH

HEAD_STEP = 2.0 * math.pi / NTH
TURN_STEP = 2.0 / NW
SCALE = TURN_LIMIT / TURN_STEP
POS = 1.0 / (SPACE_STEP * SCALE)

F32 = np.float32
HEADINGS = (np.arange(NTH, dtype=F32) * F32(HEAD_STEP)).astype(np.float64)
COSINES = [float(F32(c)) for c in np.cos(HEADINGS)]
SINES = [float(F32(s)) for s in np.sin(HEADINGS)]
TURN_TOP = float(F32((1.0 - 1.0 / NW)) / F32(HEAD_STEP))

PLANE = sorted(((a, b) for a in range(CHIP_Y) for b in range(CHIP_X) if (a, b) != (0, 0)),
               key=lambda t: -(min(t[0], CHIP_Y - t[0]) + min(t[1], CHIP_X - t[1])))


def lanes_of(g):
    return slice(g * LANES, (g + 1) * LANES)


def kernel(nx, ny, bx, by,
           drift_hbm, value_hbm, barrier_hbm, out_hbm, steps_out,
           vb, nat_v, nat_o, ob, part_a, part_b, table, drift, sent, got, rates, times,
           in_sem, ob_sem, drift_sem, out_sem, halo_send, halo_recv, max_send, max_recv):
    me_x = lax.axis_index("gx")
    me_y = lax.axis_index("gy")
    chip = me_x // CORES
    core = lax.rem(me_x, CORES)
    chip_y = chip // CHIP_X
    chip_x = lax.rem(chip, CHIP_X)
    plane = [((lax.rem(chip_y + a, CHIP_Y) * CHIP_X + lax.rem(chip_x + b, CHIP_X)) * CORES + core, me_y)
             for a, b in PLANE]
    column = []
    for k in [ny // 2] + [d for h in range(ny // 2 - 1, 0, -1) for d in (h, ny - h)] + [0]:
        for c in range(CORES - 1, -1, -1):
            if (k, c) != (0, 0):
                column.append((chip * CORES + lax.rem(core + c, CORES), lax.rem(me_y + k, ny)))
    groups = (plane, column)
    low_x, high_x = me_x > 0, me_x < nx - 1
    low_y, high_y = me_y > 0, me_y < ny - 1
    sides = ((low_x, (me_x - 1, me_y)), (high_x, (me_x + 1, me_y)),
             (low_y, (me_x, me_y - 1)), (high_y, (me_x, me_y + 1)))
    opposite = (1, 0, 3, 2)
    loads = []
    for i in range(bx):
        copy = pltpu.make_async_copy(value_hbm.at[i], nat_v.at[i], in_sem.at[i])
        copy.start()
        loads.append(copy)
    drift_copy = pltpu.make_async_copy(drift_hbm, drift, drift_sem)
    drift_copy.start()
    ob_copy = pltpu.make_async_copy(barrier_hbm, nat_o, ob_sem)
    ob_copy.start()

    ready = pltpu.get_barrier_semaphore()

    for peer in column + plane:
        pl.semaphore_signal(ready, inc=1, device_id=peer, device_id_type=MESH)
    beside_exists = jnp.where(core == 0, me_x - 1 >= 0, me_x + 1 < nx)
    beside = me_x - 1 + 2 * core

    @pl.when(beside_exists)
    def _():
        pl.semaphore_signal(ready, inc=1, device_id=(beside, me_y), device_id_type=MESH)

    lane = lax.broadcasted_iota(jnp.int32, (NTH, LANES), 1)
    low_half = lane < NW
    in_row = lax.rem(lane, NW)
    first_turn = in_row == 0
    last_turn = in_row == NW - 1
    turn_up = in_row >= NW // 2
    turning = -1.0 + (in_row.astype(jnp.float32) + 0.5) * (2.0 / NW)
    turn_w = jnp.abs(turning) * (1.0 / (HEAD_STEP * SCALE))
    zero = jnp.zeros((NTH, LANES), jnp.float32)

    heading = lax.broadcasted_iota(jnp.int32, (NTH, LANES), 0)
    cosine = jnp.full((NTH, LANES), COSINES[0], jnp.float32)
    sine = jnp.full((NTH, LANES), SINES[0], jnp.float32)
    for a in range(1, NTH):
        cosine = jnp.where(heading == a, COSINES[a], cosine)
        sine = jnp.where(heading == a, SINES[a], sine)
    for g in range(GROUPS):
        speed = SPEED_BASE + jnp.where(low_half, g, g + GROUPS).astype(jnp.float32) * SPEED_STEP
        table[0, :, lanes_of(g)] = cosine * speed * POS
        table[1, :, lanes_of(g)] = sine * speed * POS

    def split(vals):
        half = GROUPS // 2
        turned = [pltpu.roll(v, NW, 1) for v in vals]
        result = []
        for m in range(half):
            result.append(jnp.where(low_half, vals[m], turned[m + half]))
            result.append(jnp.where(low_half, turned[m], vals[m + half]))
        return result

    def joined(vals):
        half = GROUPS // 2
        turned = [pltpu.roll(v, NW, 1) for v in vals]
        return ([jnp.where(low_half, vals[2 * m], turned[2 * m + 1]) for m in range(half)]
                + [jnp.where(low_half, turned[2 * m], vals[2 * m + 1]) for m in range(half)])

    def row_slope(vals, tops):
        return tuple(
            functools.reduce(jnp.maximum, [jnp.abs(vals[g + 1] - vals[g]) for g in range(n, GROUPS - 1, len(tops))], top)
            for n, top in enumerate(tops))

    def seam_slope(step, tops):
        best = [zero, zero]
        for i in range(bx):
            for j in range(by):
                first = vb[step, i + 1, j + 1, :, lanes_of(0)]
                last = vb[step, i + 1, j + 1, :, lanes_of(GROUPS - 1)]
                best[j % 2] = jnp.maximum(best[j % 2], jnp.abs(pltpu.roll(first, NW, 1) - last))
        seam = jnp.where(low_half, jnp.maximum(best[0], best[1]), 0.0)
        return jnp.maximum(functools.reduce(jnp.maximum, tops), seam)

    for copy in loads:
        copy.wait()

    def first_rows(j, tops):
        rows = [split([nat_v[i, j, :, lanes_of(g)] for g in range(GROUPS)]) for i in range(bx)]
        for i, vals in enumerate(rows):
            for g in range(GROUPS):
                vb[0, i + 1, j + 1, :, lanes_of(g)] = vals[g]
            tops = row_slope(vals, tops)
        return tops

    top = seam_slope(0, lax.fori_loop(0, by, first_rows, (zero,) * 4))

    drift_copy.wait()
    east_ends = jnp.where(low_half, table[0, :, lanes_of(0)], table[0, :, lanes_of(GROUPS - 1)])
    north_ends = jnp.where(low_half, table[1, :, lanes_of(0)], table[1, :, lanes_of(GROUPS - 1)])
    best = [zero] * 2
    for i in range(bx):
        for j in range(by):
            both = jnp.abs(east_ends + drift[i, 0, j] * POS) + jnp.abs(north_ends + drift[i, 1, j] * POS)
            best[j % 2] = jnp.maximum(best[j % 2], both)
    rates[0] = jnp.max(jnp.maximum(best[0], best[1]))

    def split_obstacle(j, carry):
        for i in range(bx):
            vals = split([nat_o[i, j, :, lanes_of(g)] for g in range(GROUPS)])
            for g in range(GROUPS):
                ob[i, j, :, lanes_of(g)] = vals[g]
        return carry

    pl.semaphore_wait(ready, jnp.where(beside_exists, 1, 0) + len(plane) + len(column))

    def halo_copy(step, side):
        inner = {0: (1, pl.ds(1, by)), 1: (bx, pl.ds(1, by)), 2: (pl.ds(1, bx), 1), 3: (pl.ds(1, bx), by)}[side]
        outer = {0: (bx + 1, pl.ds(1, by)), 1: (0, pl.ds(1, by)), 2: (pl.ds(1, bx), by + 1), 3: (pl.ds(1, bx), 0)}[side]
        return pltpu.make_async_remote_copy(
            src_ref=vb.at[(step,) + inner], dst_ref=vb.at[(step,) + outer],
            send_sem=halo_send.at[step, side], recv_sem=halo_recv.at[step, side],
            device_id=sides[side][1], device_id_type=MESH)

    def ghost(step, side):
        if side < 2:
            to, near, far = ((0, 1, 2), (bx + 1, bx, bx - 1))[side]

            def fill(j, carry):
                vb[step, to, j] = 2.0 * vb[step, near, j] - vb[step, far, j]
                return carry

            lax.fori_loop(1, by + 1, fill, 0)
        else:
            to, near, far = ((0, 1, 2), (by + 1, by, by - 1))[side - 2]

            def fill(i, carry):
                vb[step, i, to] = 2.0 * vb[step, i, near] - vb[step, i, far]
                return carry

            lax.fori_loop(1, bx + 1, fill, 0)

    def spread(step, stage):
        for k, peer in enumerate(groups[stage]):
            pltpu.make_async_remote_copy(
                src_ref=sent.at[step, stage], dst_ref=got.at[step, stage, k],
                send_sem=max_send.at[step, stage], recv_sem=max_recv.at[step, stage],
                device_id=peer, device_id_type=MESH).start()

    def wait_all(step, stage, sem):
        pltpu.make_async_copy(got.at[step, stage], got.at[step, stage], sem.at[step, stage]).wait()

    def largest(step, stage, at):
        best = [sent[step, stage, at]] + [got[step, stage, k, at] for k in range(len(groups[stage]))]
        while len(best) > 1:
            best = [jnp.maximum(a, b) for a, b in zip(best[::2], best[1::2])] + best[len(best) // 2 * 2:]
        return best[0]

    def inner_terms(step):
        def row(i, j):
            vals = [vb[step, i, j, :, lanes_of(g)] for g in range(GROUPS)]
            seam_up = pltpu.roll(vals[0], NW, 1)
            seam_down = pltpu.roll(vals[GROUPS - 1], NW, 1)
            for g in range(GROUPS):
                v = vals[g]
                ahead = vals[g + 1] - v if g < GROUPS - 1 else seam_up - v
                behind = vals[g - 1] - v if g > 0 else seam_down - v
                if g == 0:
                    behind = jnp.where(low_half, -ahead, behind)
                if g == GROUPS - 1:
                    ahead = jnp.where(low_half, ahead, -behind)
                span = ahead - behind
                part_b[i - 1, j - 1, :, lanes_of(g)] = ahead + behind
                acc = span * span * (1.0 / (4.0 * SPEED_STEP * SPEED_STEP * 2.0 * EFFORT_COST * SCALE))
                right = pltpu.roll(v, LANES - 1, 1) - v
                left = pltpu.roll(v, 1, 1) - v
                acc += jnp.maximum(jnp.where(last_turn, -left, right), jnp.where(first_turn, -right, left))
                around = jnp.where(turn_up, pltpu.roll(v, NTH - 1, 0), pltpu.roll(v, 1, 0))
                acc += turn_w * (around - v)
                part_a[i - 1, j - 1, :, lanes_of(g)] = acc

        return row

    def position_terms(step):
        def row(i, j):
            dx = drift[i - 1, 0, j - 1] * POS
            dy = drift[i - 1, 1, j - 1] * POS
            for g in range(GROUPS):
                s = lanes_of(g)
                v = vb[step, i, j, :, s]
                east = table[0, :, s] + dx
                north = table[1, :, s] + dy
                from_x = jnp.where(east > 0.0, vb[step, i + 1, j, :, s], vb[step, i - 1, j, :, s])
                from_y = jnp.where(north > 0.0, vb[step, i, j + 1, :, s], vb[step, i, j - 1, :, s])
                part_a[i - 1, j - 1, :, s] += jnp.abs(east) * (from_x - v) + jnp.abs(north) * (from_y - v)

        return row

    def each(first, last, rows):
        def body(j, carry):
            rows(j)
            return carry

        lax.fori_loop(first, last, body, 0)

    def send_halos(step, two):
        for side in two:
            @pl.when(sides[side][0])
            def _(side=side):
                halo_copy(step, side).start()

    def take_halos(step, two):
        for side in two:
            @pl.when(jnp.logical_not(sides[side][0]))
            def _(side=side):
                ghost(step, side)

            @pl.when(sides[side][0])
            def _(side=side):
                halo_copy(step, opposite[side]).wait_recv()

    def share(step, top):
        inner, position = inner_terms(step), position_terms(step)
        sent[step, 0, 0] = jnp.max(top)
        sent[step, 0, 1] = rates[0]
        spread(step, 0)
        send_halos(step, (2, 3))

        def inner_rows(planes):
            def rows(j):
                for i in planes:
                    inner(i, j)

            return rows

        each(1, by + 1, inner_rows(range(1, bx // 2 + 1)))
        send_halos(step, (0, 1))
        each(1, by + 1, inner_rows(range(bx // 2 + 1, bx + 1)))
        wait_all(step, 0, max_recv)
        sent[step, 1, 0] = largest(step, 0, 0)

        @pl.when(step == 0)
        def _():
            rates[0] = largest(step, 0, 1)

        sent[step, 1, 1] = rates[0]
        spread(step, 1)

        @pl.when(step == 0)
        def _():
            ob_copy.wait()
            each(0, by, lambda j: split_obstacle(j, 0))

        take_halos(step, (2, 3))

        def middle(j):
            for i in range(2, bx):
                position(i, j)

        each(1, by + 1, middle)
        take_halos(step, (0, 1))

        def rims(j):
            for i in (1, bx):
                position(i, j)

        each(1, by + 1, rims)

    def weights(step):
        wait_all(step, 1, max_recv)
        slope = largest(step, 1, 0)

        @pl.when(step == 0)
        def _():
            rates[0] = largest(step, 1, 1)

        top_slope = jnp.full((NTH, LANES), slope, jnp.float32) * (1.0 / SPEED_STEP)
        rate_top = jnp.full((NTH, LANES), rates[0], jnp.float32) * SCALE + TURN_TOP + SCALE
        dt = COURANT / (rate_top + top_slope * (1.0 / (EFFORT_COST * SPEED_STEP)))
        times[step] = dt
        return SCALE * dt, dt * top_slope * (0.5 / (SPEED_STEP * EFFORT_COST))

    def one_step(step, top):
        share(step, top)
        weight_a, weight_b = weights(step)

        def update(j, tops):
            for i in range(bx):
                vals = []
                for g in range(GROUPS):
                    s = lanes_of(g)
                    moved = vb[step, i + 1, j + 1, :, s] + weight_a * part_a[i, j, :, s] + weight_b * part_b[i, j, :, s]
                    moved = jnp.minimum(moved, ob[i, j, :, s])
                    vb[step + 1, i + 1, j + 1, :, s] = moved
                    vals.append(moved)
                tops = row_slope(vals, tops)
            return tops

        tops = lax.fori_loop(0, by, update, (zero,) * 4)
        return seam_slope(step + 1, tops)

    top = lax.fori_loop(0, ITERS - 1, one_step, top)
    last = ITERS - 1
    share(last, top)

    weight_a, weight_b = weights(last)
    stores = []
    half = by // 2
    for i in range(bx):
        def final(part, carry, i=i):
            for n in range(half):
                j = part * half + n
                vals = []
                for g in range(GROUPS):
                    s = lanes_of(g)
                    vals.append(vb[last, i + 1, j + 1, :, s] + weight_a * part_a[i, j, :, s] + weight_b * part_b[i, j, :, s])
                for g, moved in enumerate(joined(vals)):
                    ob[i, j, :, lanes_of(g)] = jnp.minimum(moved, nat_o[i, j, :, lanes_of(g)])
            return carry

        lax.fori_loop(0, 2, final, 0)
        copy = pltpu.make_async_copy(ob.at[i], out_hbm.at[i], out_sem.at[i])
        copy.start()
        stores.append(copy)

    for step in range(ITERS):
        steps_out[step] = jnp.max(times[step])

    def finish(step, carry):
        for stage in range(2):
            wait_all(step, stage, max_send)
        for side in range(4):
            @pl.when(sides[side][0])
            def _(side=side):
                halo_copy(step, side).wait_send()
        return carry

    lax.fori_loop(0, ITERS, finish, 0)
    for copy in stores:
        copy.wait()


def per_device(nx, ny, value_field, obstacle, drift_field):
    bx, by = value_field.shape[:2]
    shape = value_field.shape
    hbm = pl.BlockSpec(memory_space=pltpu.MemorySpace.HBM)
    dma = pltpu.SemaphoreType.DMA
    block = pltpu.VMEM(shape, jnp.float32)
    return pl.pallas_call(
        functools.partial(kernel, nx, ny, bx, by),
        out_shape=(jax.ShapeDtypeStruct(shape, jnp.float32), jax.ShapeDtypeStruct((ITERS,), jnp.float32)),
        in_specs=[hbm, hbm, hbm],
        out_specs=(pl.BlockSpec(memory_space=pl.ANY), pl.BlockSpec(memory_space=pltpu.SMEM)),
        scratch_shapes=[
            pltpu.VMEM((ITERS, bx + 2, by + 2) + shape[2:], jnp.float32),
            block, block, block, block, block,
            pltpu.VMEM((2,) + shape[2:], jnp.float32),
            pltpu.SMEM((bx, 2, by), jnp.float32),
            pltpu.SMEM((ITERS, 2, 8), jnp.float32),
            pltpu.SMEM((ITERS, 2, len(PLANE), 8), jnp.float32),
            pltpu.SMEM((1,), jnp.float32),
            pltpu.VMEM((ITERS, NTH, LANES), jnp.float32),
            dma((bx,)), dma, dma, dma((bx,)),
            dma((ITERS, 4)), dma((ITERS, 4)), dma((ITERS, 2)), dma((ITERS, 2)),
        ],
        compiler_params=pltpu.CompilerParams(
            collective_id=0, has_side_effects=True, vmem_limit_bytes=52 * 1024 * 1024),
        name="safe_set_steps",
    )(jnp.transpose(drift_field, (0, 2, 1)), value_field, obstacle)


def solution(mesh):
    nx, ny = mesh.shape["gx"], mesh.shape["gy"]
    placed = (P("gx", "gy", None, None), P("gx", "gy", None, None), P("gx", "gy", None))
    return jax.shard_map(
        functools.partial(per_device, nx, ny),
        mesh=mesh,
        in_specs=placed,
        out_specs=(P("gx", "gy", None, None), P()),
        check_vma=False,
    )
```

time: 64.5 us -> 55.4 us (0.86)
  Pallas kernels: 57.4 us -> 52.5 us
  local copies, waits for them, and re-layouts: 6.23 us -> 2.16 us
    pallas_call x1, Pallas kernels: 57.4 us -> 52.5 us  [per_device(): pl.pallas_call(functools.partial(kernel, nx, ny, bx, by), out_shape=(jax....]
    unnamed x11 -> x4, local copies, waits for them, and re-layouts: 6.15 us -> 2.16 us
where the time goes in v2:
time: 55.4 us; the launch traced here: 55.3 us
  Pallas kernels  52.5 us (95%)
  local copies, waits for them, and re-layouts  2.16 us (4%)
  between operations  0.65 us (1%)
    pallas_call x1, Pallas kernels, per_device(): pl.pallas_call(functools.partial(kernel, nx, ny, bx, by), out_shape=(jax....  52.5 us
    unnamed x4, local copies, waits for them, and re-layouts  2.16 us

profile of v2, /device:TPU:1, one launch (start us, length us, event | category | flops | bytes accessed | tf_op | source)
XLA Modules:
  0.0 55.3 jit_solution(2962028834631978124)
XLA Ops:
  0.6 0.0 copy-start
  0.6 0.7 %copy-done = f32[4,8,2]{1,2,0:T(2,128)S(1)} copy-done((f32[4,8,2]{1,2,0:T(2,128)S(1)}, f32[4,8,2]{1,2,0:T(2,128)}, u32[]{:S(2)}) %copy-start) | copy-done | bytes 280
  1.3 52.5 %safe_set_steps.1 = (f32[4,8,8,1024]{3,2,1,0:T(8,128)S(1)}, f32[4]{0:T(128)S(1)}) custom-call(f32[4,2,8]{2,1,0:T(2,128)S(1)} %bitcast.1, f32[4,8,8,1024]{3,2,1,0:T(8,128)} %value_hbm.1, f32[4,8,8,1024]{3,2,1,0:T(8,128)} %barrier_hbm.1), custom_call_target="tpu_custom_call" | custom-call | tf_op jit(solution)/shard_map/safe_set_steps/pallas_call | solution.py:408
  53.8 1.0 %copy.7 = f32[4,8,8,1024]{3,2,1,0:T(8,128)} copy(f32[4,8,8,1024]{3,2,1,0:T(8,128)S(1)} %get-tuple-element.4) | data formatting | bytes 2097152
  54.8 0.5 copy.8
Async XLA Ops:
  0.6 0.7 %copy-start = (f32[4,8,2]{1,2,0:T(2,128)S(1)}, f32[4,8,2]{1,2,0:T(2,128)}, u32[]{:S(2)}) copy-start(f32[4,8,2]{1,2,0:T(2,128)} %param.5) | copy-start | bytes 772

commit v3 on v2

--- a/solution.py
+++ b/solution.py
@@ -38,7 +38,7 @@
 SINES = [float(F32(s)) for s in np.sin(HEADINGS)]
 TURN_TOP = float(F32((1.0 - 1.0 / NW)) / F32(HEAD_STEP))
 
-PLANE = sorted(((a, b) for a in range(CHIP_Y) for b in range(CHIP_X) if (a, b) != (0, 0)),
+PLANE = sorted(((a, b) for a in range(CHIP_Y) for b in range(CHIP_X)),
                key=lambda t: -(min(t[0], CHIP_Y - t[0]) + min(t[1], CHIP_X - t[1])))
 
 
@@ -48,27 +48,40 @@
 
 def kernel(nx, ny, bx, by,
            drift_hbm, value_hbm, barrier_hbm, out_hbm, steps_out,
-           vb, nat_v, nat_o, ob, part_a, part_b, table, drift, sent, got, rates, times,
-           in_sem, ob_sem, drift_sem, out_sem, halo_send, halo_recv, max_send, max_recv):
+           vb, nat_v, nat_o, ob, part_a, part_b, table, drift, pair, sent, got, rates, times, held,
+           in_sem, ob_sem, drift_sem, out_sem, halo_send, halo_recv,
+           pair_send, pair_recv, max_send, max_recv):
     me_x = lax.axis_index("gx")
     me_y = lax.axis_index("gy")
     chip = me_x // CORES
     core = lax.rem(me_x, CORES)
     chip_y = chip // CHIP_X
     chip_x = lax.rem(chip, CHIP_X)
-    plane = [((lax.rem(chip_y + a, CHIP_Y) * CHIP_X + lax.rem(chip_x + b, CHIP_X)) * CORES + core, me_y)
-             for a, b in PLANE]
-    column = []
-    for k in [ny // 2] + [d for h in range(ny // 2 - 1, 0, -1) for d in (h, ny - h)] + [0]:
-        for c in range(CORES - 1, -1, -1):
-            if (k, c) != (0, 0):
-                column.append((chip * CORES + lax.rem(core + c, CORES), lax.rem(me_y + k, ny)))
-    groups = (plane, column)
+    partner = (chip * CORES + 1 - core, me_y)
+    plane = [(lax.rem(chip_y + a, CHIP_Y) * CHIP_X + lax.rem(chip_x + b, CHIP_X)) * CORES + core for a, b in PLANE]
+    others = ny * len(PLANE) - 1
     low_x, high_x = me_x > 0, me_x < nx - 1
     low_y, high_y = me_y > 0, me_y < ny - 1
     sides = ((low_x, (me_x - 1, me_y)), (high_x, (me_x + 1, me_y)),
              (low_y, (me_x, me_y - 1)), (high_y, (me_x, me_y + 1)))
     opposite = (1, 0, 3, 2)
+    def layer(k):
+        half = (k + 1) // 2
+        return lax.rem(me_y + ny // 2 + half * (2 * lax.rem(k, 2) - 1) + ny, ny)
+
+    def for_others(act):
+        def body(k, carry):
+            z = layer(k)
+            for n, gx in enumerate(plane):
+                run = functools.partial(act, k * len(plane) + n, (gx, z))
+                if n == len(plane) - 1:
+                    pl.when(k < ny - 1)(run)
+                else:
+                    run()
+            return carry
+
+        lax.fori_loop(0, ny, body, 0)
+
     loads = []
     for i in range(bx):
         copy = pltpu.make_async_copy(value_hbm.at[i], nat_v.at[i], in_sem.at[i])
@@ -81,8 +94,11 @@
 
     ready = pltpu.get_barrier_semaphore()
 
-    for peer in column + plane:
+    def greet(n, peer):
         pl.semaphore_signal(ready, inc=1, device_id=peer, device_id_type=MESH)
+
+    for_others(greet)
+    greet(0, partner)
     beside_exists = jnp.where(core == 0, me_x - 1 >= 0, me_x + 1 < nx)
     beside = me_x - 1 + 2 * core
 
@@ -168,18 +184,30 @@
         for i in range(bx):
             vals = split([nat_o[i, j, :, lanes_of(g)] for g in range(GROUPS)])
             for g in range(GROUPS):
-                ob[i, j, :, lanes_of(g)] = vals[g]
+                ob[i + 1, j + 1, :, lanes_of(g)] = vals[g]
         return carry
 
-    pl.semaphore_wait(ready, jnp.where(beside_exists, 1, 0) + len(plane) + len(column))
-
-    def halo_copy(step, side):
+    pl.semaphore_wait(ready, jnp.where(beside_exists, 1, 0) + others + 1)
+
+    def rim_copy(ref, at, side):
         inner = {0: (1, pl.ds(1, by)), 1: (bx, pl.ds(1, by)), 2: (pl.ds(1, bx), 1), 3: (pl.ds(1, bx), by)}[side]
         outer = {0: (bx + 1, pl.ds(1, by)), 1: (0, pl.ds(1, by)), 2: (pl.ds(1, bx), by + 1), 3: (pl.ds(1, bx), 0)}[side]
         return pltpu.make_async_remote_copy(
-            src_ref=vb.at[(step,) + inner], dst_ref=vb.at[(step,) + outer],
-            send_sem=halo_send.at[step, side], recv_sem=halo_recv.at[step, side],
+            src_ref=ref.at[inner], dst_ref=ref.at[outer],
+            send_sem=halo_send.at[at, side], recv_sem=halo_recv.at[at, side],
             device_id=sides[side][1], device_id_type=MESH)
+
+    def send_rims(ref, at):
+        for side in (2, 3, 0, 1):
+            @pl.when(sides[side][0])
+            def _(side=side):
+                rim_copy(ref, at, side).start()
+
+    def take_rims(ref, at):
+        for side in range(4):
+            @pl.when(sides[side][0])
+            def _(side=side):
+                rim_copy(ref, at, opposite[side]).wait_recv()
 
     def ghost(step, side):
         if side < 2:
@@ -199,35 +227,50 @@
 
             lax.fori_loop(1, bx + 1, fill, 0)
 
-    def spread(step, stage):
-        for k, peer in enumerate(groups[stage]):
+    def pair_copy(step):
+        return pltpu.make_async_remote_copy(
+            src_ref=pair.at[step, 0], dst_ref=pair.at[step, 1],
+            send_sem=pair_send.at[step], recv_sem=pair_recv.at[step],
+            device_id=partner, device_id_type=MESH)
+
+    def spread(step):
+        def send(n, peer):
             pltpu.make_async_remote_copy(
-                src_ref=sent.at[step, stage], dst_ref=got.at[step, stage, k],
-                send_sem=max_send.at[step, stage], recv_sem=max_recv.at[step, stage],
+                src_ref=sent.at[step], dst_ref=got.at[step, n],
+                send_sem=max_send.at[step], recv_sem=max_recv.at[step],
                 device_id=peer, device_id_type=MESH).start()
 
-    def wait_all(step, stage, sem):
-        pltpu.make_async_copy(got.at[step, stage], got.at[step, stage], sem.at[step, stage]).wait()
-
-    def largest(step, stage, at):
-        best = [sent[step, stage, at]] + [got[step, stage, k, at] for k in range(len(groups[stage]))]
-        while len(best) > 1:
-            best = [jnp.maximum(a, b) for a, b in zip(best[::2], best[1::2])] + best[len(best) // 2 * 2:]
-        return best[0]
+        for_others(send)
+
+    def wait_all(step, sem):
+        rows = got.at[step, pl.ds(0, others)]
+        pltpu.make_async_copy(rows, rows, sem.at[step]).wait()
+
+    def largest(step, at):
+        best = [sent[step, at]] + [got[step, n, at] for n in range(3)]
+        for n in range(3, others):
+            best[n % 4] = jnp.maximum(best[n % 4], got[step, n, at])
+        return jnp.maximum(jnp.maximum(best[0], best[1]), jnp.maximum(best[2], best[3]))
+
+    def speed_sides(vals):
+        seam_up = pltpu.roll(vals[0], NW, 1)
+        seam_down = pltpu.roll(vals[GROUPS - 1], NW, 1)
+        result = []
+        for g, v in enumerate(vals):
+            ahead = vals[g + 1] - v if g < GROUPS - 1 else seam_up - v
+            behind = vals[g - 1] - v if g > 0 else seam_down - v
+            if g == 0:
+                behind = jnp.where(low_half, -ahead, behind)
+            if g == GROUPS - 1:
+                ahead = jnp.where(low_half, ahead, -behind)
+            result.append((ahead, behind))
+        return result
 
     def inner_terms(step):
         def row(i, j):
             vals = [vb[step, i, j, :, lanes_of(g)] for g in range(GROUPS)]
-            seam_up = pltpu.roll(vals[0], NW, 1)
-            seam_down = pltpu.roll(vals[GROUPS - 1], NW, 1)
-            for g in range(GROUPS):
+            for g, (ahead, behind) in enumerate(speed_sides(vals)):
                 v = vals[g]
-                ahead = vals[g + 1] - v if g < GROUPS - 1 else seam_up - v
-                behind = vals[g - 1] - v if g > 0 else seam_down - v
-                if g == 0:
-                    behind = jnp.where(low_half, -ahead, behind)
-                if g == GROUPS - 1:
-                    ahead = jnp.where(low_half, ahead, -behind)
                 span = ahead - behind
                 part_b[i - 1, j - 1, :, lanes_of(g)] = ahead + behind
                 acc = span * span * (1.0 / (4.0 * SPEED_STEP * SPEED_STEP * 2.0 * EFFORT_COST * SCALE))
@@ -236,7 +279,7 @@
                 acc += jnp.maximum(jnp.where(last_turn, -left, right), jnp.where(first_turn, -right, left))
                 around = jnp.where(turn_up, pltpu.roll(v, NTH - 1, 0), pltpu.roll(v, 1, 0))
                 acc += turn_w * (around - v)
-                part_a[i - 1, j - 1, :, lanes_of(g)] = acc
+                part_a[step, i, j, :, lanes_of(g)] = acc
 
         return row
 
@@ -251,7 +294,7 @@
                 north = table[1, :, s] + dy
                 from_x = jnp.where(east > 0.0, vb[step, i + 1, j, :, s], vb[step, i - 1, j, :, s])
                 from_y = jnp.where(north > 0.0, vb[step, i, j + 1, :, s], vb[step, i, j - 1, :, s])
-                part_a[i - 1, j - 1, :, s] += jnp.abs(east) * (from_x - v) + jnp.abs(north) * (from_y - v)
+                part_a[step, i, j, :, s] += jnp.abs(east) * (from_x - v) + jnp.abs(north) * (from_y - v)
 
         return row
 
@@ -262,28 +305,38 @@
 
         lax.fori_loop(first, last, body, 0)
 
-    def send_halos(step, two):
-        for side in two:
+    def halo_row(step, i, j):
+        before = step - 1
+        vals = [vb[before, i, j, :, lanes_of(g)] for g in range(GROUPS)]
+        for g, (ahead, behind) in enumerate(speed_sides(vals)):
+            s = lanes_of(g)
+            moved = vals[g] + held[0] * part_a[before, i, j, :, s] + held[1] * (ahead + behind)
+            vb[step, i, j, :, s] = jnp.minimum(moved, ob[i, j, :, s])
+
+    def halo_rows(step):
+        for side, i in ((0, 0), (1, bx + 1)):
             @pl.when(sides[side][0])
-            def _(side=side):
-                halo_copy(step, side).start()
-
-    def take_halos(step, two):
-        for side in two:
-            @pl.when(jnp.logical_not(sides[side][0]))
-            def _(side=side):
-                ghost(step, side)
-
+            def _(i=i):
+                def pair_of_rows(n):
+                    halo_row(step, i, 2 * n + 1)
+                    halo_row(step, i, 2 * n + 2)
+
+                each(0, by // 2, pair_of_rows)
+
+        for side, j in ((2, 0), (3, by + 1)):
             @pl.when(sides[side][0])
-            def _(side=side):
-                halo_copy(step, opposite[side]).wait_recv()
+            def _(j=j):
+                def pair_of_rows(n):
+                    halo_row(step, 2 * n + 1, j)
+                    halo_row(step, 2 * n + 2, j)
+
+                each(0, bx // 2, pair_of_rows)
 
     def share(step, top):
         inner, position = inner_terms(step), position_terms(step)
-        sent[step, 0, 0] = jnp.max(top)
-        sent[step, 0, 1] = rates[0]
-        spread(step, 0)
-        send_halos(step, (2, 3))
+        pair[step, 0, 0] = jnp.max(top)
+        pair[step, 0, 1] = rates[0]
+        pair_copy(step).start()
 
         def inner_rows(planes):
             def rows(j):
@@ -292,70 +345,93 @@
 
             return rows
 
-        each(1, by + 1, inner_rows(range(1, bx // 2 + 1)))
-        send_halos(step, (0, 1))
-        each(1, by + 1, inner_rows(range(bx // 2 + 1, bx + 1)))
-        wait_all(step, 0, max_recv)
-        sent[step, 1, 0] = largest(step, 0, 0)
+        each(1, 2, inner_rows(range(1, bx + 1)))
+        pair_copy(step).wait_recv()
+        sent[step, 0] = jnp.maximum(pair[step, 0, 0], pair[step, 1, 0])
+        sent[step, 1] = jnp.maximum(pair[step, 0, 1], pair[step, 1, 1])
+        spread(step)
 
         @pl.when(step == 0)
         def _():
-            rates[0] = largest(step, 0, 1)
-
-        sent[step, 1, 1] = rates[0]
-        spread(step, 1)
+            send_rims(vb.at[0], 0)
+
+        each(2, by + 1, inner_rows(range(1, bx + 1)))
 
         @pl.when(step == 0)
         def _():
             ob_copy.wait()
             each(0, by, lambda j: split_obstacle(j, 0))
-
-        take_halos(step, (2, 3))
-
-        def middle(j):
+            send_rims(ob, ITERS)
+            take_rims(vb.at[0], 0)
+
+        @pl.when(step == 1)
+        def _():
+            take_rims(ob, ITERS)
+
+        @pl.when(step > 0)
+        def _():
+            take_rims(part_a.at[step - 1], step)
+            halo_rows(step)
+
+        for side in range(4):
+            @pl.when(jnp.logical_not(sides[side][0]))
+            def _(side=side):
+                ghost(step, side)
+
+        def x_rims(j):
+            position(1, j)
+            position(bx, j)
+
+        def y_rims(i):
+            position(i, 1)
+            position(i, by)
+
+        def inside(j):
             for i in range(2, bx):
                 position(i, j)
 
-        each(1, by + 1, middle)
-        take_halos(step, (0, 1))
-
-        def rims(j):
-            for i in (1, bx):
-                position(i, j)
-
-        each(1, by + 1, rims)
+        each(1, by + 1, x_rims)
+        each(2, bx, y_rims)
+
+        @pl.when(step < ITERS - 1)
+        def _():
+            send_rims(part_a.at[step], step + 1)
+
+        each(2, by, inside)
 
     def weights(step):
-        wait_all(step, 1, max_recv)
-        slope = largest(step, 1, 0)
+        wait_all(step, max_recv)
+        slope = largest(step, 0)
 
         @pl.when(step == 0)
         def _():
-            rates[0] = largest(step, 1, 1)
+            rates[0] = largest(step, 1)
 
         top_slope = jnp.full((NTH, LANES), slope, jnp.float32) * (1.0 / SPEED_STEP)
         rate_top = jnp.full((NTH, LANES), rates[0], jnp.float32) * SCALE + TURN_TOP + SCALE
         dt = COURANT / (rate_top + top_slope * (1.0 / (EFFORT_COST * SPEED_STEP)))
         times[step] = dt
-        return SCALE * dt, dt * top_slope * (0.5 / (SPEED_STEP * EFFORT_COST))
+        held[0] = SCALE * dt
+        held[1] = dt * top_slope * (0.5 / (SPEED_STEP * EFFORT_COST))
+        return held[0], held[1]
 
     def one_step(step, top):
         share(step, top)
         weight_a, weight_b = weights(step)
 
         def update(j, tops):
-            for i in range(bx):
+            for i in range(1, bx + 1):
                 vals = []
                 for g in range(GROUPS):
                     s = lanes_of(g)
-                    moved = vb[step, i + 1, j + 1, :, s] + weight_a * part_a[i, j, :, s] + weight_b * part_b[i, j, :, s]
+                    moved = vb[step, i, j, :, s] + weight_a * part_a[step, i, j, :, s] + weight_b * part_b[i - 1, j - 1, :, s]
                     moved = jnp.minimum(moved, ob[i, j, :, s])
-                    vb[step + 1, i + 1, j + 1, :, s] = moved
+                    vb[step + 1, i, j, :, s] = moved
                     vals.append(moved)
                 tops = row_slope(vals, tops)
             return tops
 
-        tops = lax.fori_loop(0, by, update, (zero,) * 4)
+        tops = lax.fori_loop(1, by + 1, update, (zero,) * 4)
         return seam_slope(step + 1, tops)
 
     top = lax.fori_loop(0, ITERS - 1, one_step, top)
@@ -372,13 +448,14 @@
                 vals = []
                 for g in range(GROUPS):
                     s = lanes_of(g)
-                    vals.append(vb[last, i + 1, j + 1, :, s] + weight_a * part_a[i, j, :, s] + weight_b * part_b[i, j, :, s])
+                    vals.append(vb[last, i + 1, j + 1, :, s] + weight_a * part_a[last, i + 1, j + 1, :, s]
+                                + weight_b * part_b[i, j, :, s])
                 for g, moved in enumerate(joined(vals)):
-                    ob[i, j, :, lanes_of(g)] = jnp.minimum(moved, nat_o[i, j, :, lanes_of(g)])
+                    nat_v[i, j, :, lanes_of(g)] = jnp.minimum(moved, nat_o[i, j, :, lanes_of(g)])
             return carry
 
         lax.fori_loop(0, 2, final, 0)
-        copy = pltpu.make_async_copy(ob.at[i], out_hbm.at[i], out_sem.at[i])
+        copy = pltpu.make_async_copy(nat_v.at[i], out_hbm.at[i], out_sem.at[i])
         copy.start()
         stores.append(copy)
 
@@ -386,15 +463,20 @@
         steps_out[step] = jnp.max(times[step])
 
     def finish(step, carry):
-        for stage in range(2):
-            wait_all(step, stage, max_send)
+        pair_copy(step).wait_send()
+        wait_all(step, max_send)
+        return carry
+
+    lax.fori_loop(0, ITERS, finish, 0)
+
+    def rims_sent(at, carry):
         for side in range(4):
             @pl.when(sides[side][0])
             def _(side=side):
-                halo_copy(step, side).wait_send()
+                rim_copy(ob, at, side).wait_send()
         return carry
 
-    lax.fori_loop(0, ITERS, finish, 0)
+    lax.fori_loop(0, ITERS + 1, rims_sent, 0)
     for copy in stores:
         copy.wait()
 
@@ -412,15 +494,20 @@
         out_specs=(pl.BlockSpec(memory_space=pl.ANY), pl.BlockSpec(memory_space=pltpu.SMEM)),
         scratch_shapes=[
             pltpu.VMEM((ITERS, bx + 2, by + 2) + shape[2:], jnp.float32),
-            block, block, block, block, block,
+            block, block,
+            pltpu.VMEM((bx + 2, by + 2) + shape[2:], jnp.float32),
+            pltpu.VMEM((ITERS, bx + 2, by + 2) + shape[2:], jnp.float32),
+            block,
             pltpu.VMEM((2,) + shape[2:], jnp.float32),
             pltpu.SMEM((bx, 2, by), jnp.float32),
             pltpu.SMEM((ITERS, 2, 8), jnp.float32),
-            pltpu.SMEM((ITERS, 2, len(PLANE), 8), jnp.float32),
+            pltpu.SMEM((ITERS, 8), jnp.float32),
+            pltpu.SMEM((ITERS, ny * len(PLANE) - 1, 8), jnp.float32),
             pltpu.SMEM((1,), jnp.float32),
             pltpu.VMEM((ITERS, NTH, LANES), jnp.float32),
+            pltpu.VMEM((2, NTH, LANES), jnp.float32),
             dma((bx,)), dma, dma, dma((bx,)),
-            dma((ITERS, 4)), dma((ITERS, 4)), dma((ITERS, 2)), dma((ITERS, 2)),
+            dma((ITERS + 1, 4)), dma((ITERS + 1, 4)), dma((ITERS,)), dma((ITERS,)), dma((ITERS,)), dma((ITERS,)),
         ],
         compiler_params=pltpu.CompilerParams(
             collective_id=0, has_side_effects=True, vmem_limit_bytes=52 * 1024 * 1024),

time: 55.4 us -> 53.3 us (0.962)
  Pallas kernels: 52.5 us -> 50.3 us
    pallas_call x1, Pallas kernels: 52.5 us -> 50.3 us  [per_device(): pl.pallas_call(functools.partial(kernel, nx, ny, bx, by), out_shape=(jax....]
where the time goes in v3:
time: 53.3 us; the launch traced here: 53.2 us
  Pallas kernels  50.3 us (94%)
  local copies, waits for them, and re-layouts  2.16 us (4%)
  between operations  0.65 us (1%)
    pallas_call x1, Pallas kernels, per_device(): pl.pallas_call(functools.partial(kernel, nx, ny, bx, by), out_shape=(jax....  50.3 us
    unnamed x4, local copies, waits for them, and re-layouts  2.16 us

profile of v3, /device:TPU:1, one launch (start us, length us, event | category | flops | bytes accessed | tf_op | source)
XLA Modules:
  0.0 53.2 jit_solution(2391026717812842001)
XLA Ops:
  0.6 0.0 copy-start
  0.6 0.7 %copy-done = f32[4,8,2]{1,2,0:T(2,128)S(1)} copy-done((f32[4,8,2]{1,2,0:T(2,128)S(1)}, f32[4,8,2]{1,2,0:T(2,128)}, u32[]{:S(2)}) %copy-start) | copy-done | bytes 280
  1.3 50.3 %safe_set_steps.1 = (f32[4,8,8,1024]{3,2,1,0:T(8,128)S(1)}, f32[4]{0:T(128)S(1)}) custom-call(f32[4,2,8]{2,1,0:T(2,128)S(1)} %bitcast.1, f32[4,8,8,1024]{3,2,1,0:T(8,128)} %value_hbm.1, f32[4,8,8,1024]{3,2,1,0:T(8,128)} %barrier_hbm.1), custom_call_target="tpu_custom_call" | custom-call | tf_op jit(solution)/shard_map/safe_set_steps/pallas_call | solution.py:490
  51.7 1.0 %copy.7 = f32[4,8,8,1024]{3,2,1,0:T(8,128)} copy(f32[4,8,8,1024]{3,2,1,0:T(8,128)S(1)} %get-tuple-element.4) | data formatting | bytes 2097152
  52.6 0.5 copy.8
Async XLA Ops:
  0.6 0.7 %copy-start = (f32[4,8,2]{1,2,0:T(2,128)S(1)}, f32[4,8,2]{1,2,0:T(2,128)}, u32[]{:S(2)}) copy-start(f32[4,8,2]{1,2,0:T(2,128)} %param.5) | copy-start | bytes 772

commit v4 on v3

--- a/solution.py
+++ b/solution.py
@@ -227,6 +227,8 @@
 
             lax.fori_loop(1, bx + 1, fill, 0)
 
+    send_rims(vb.at[0], 0)
+
     def pair_copy(step):
         return pltpu.make_async_remote_copy(
             src_ref=pair.at[step, 0], dst_ref=pair.at[step, 1],
@@ -345,17 +347,22 @@
 
             return rows
 
-        each(1, 2, inner_rows(range(1, bx + 1)))
+        def y_rim_rows(n):
+            for i in range(1, bx + 1):
+                inner(i, n * (by - 1) + 1)
+
+        def x_rim_rows(j):
+            inner(1, j)
+            inner(bx, j)
+
+        each(0, 2, y_rim_rows)
+        each(2, 4, x_rim_rows)
         pair_copy(step).wait_recv()
         sent[step, 0] = jnp.maximum(pair[step, 0, 0], pair[step, 1, 0])
         sent[step, 1] = jnp.maximum(pair[step, 0, 1], pair[step, 1, 1])
         spread(step)
 
-        @pl.when(step == 0)
-        def _():
-            send_rims(vb.at[0], 0)
-
-        each(2, by + 1, inner_rows(range(1, bx + 1)))
+        each(4, by, x_rim_rows)
 
         @pl.when(step == 0)
         def _():
@@ -397,6 +404,7 @@
         def _():
             send_rims(part_a.at[step], step + 1)
 
+        each(2, by, inner_rows(range(2, bx)))
         each(2, by, inside)
 
     def weights(step):
@@ -419,8 +427,8 @@
         share(step, top)
         weight_a, weight_b = weights(step)
 
-        def update(j, tops):
-            for i in range(1, bx + 1):
+        def update(n, tops):
+            for i, j in [(i, 2 * n + m) for m in (1, 2) for i in range(1, bx + 1)]:
                 vals = []
                 for g in range(GROUPS):
                     s = lanes_of(g)
@@ -431,7 +439,7 @@
                 tops = row_slope(vals, tops)
             return tops
 
-        tops = lax.fori_loop(1, by + 1, update, (zero,) * 4)
+        tops = lax.fori_loop(0, by // 2, update, (zero,) * 4)
         return seam_slope(step + 1, tops)
 
     top = lax.fori_loop(0, ITERS - 1, one_step, top)
@@ -512,7 +520,7 @@
         compiler_params=pltpu.CompilerParams(
             collective_id=0, has_side_effects=True, vmem_limit_bytes=52 * 1024 * 1024),
         name="safe_set_steps",
-    )(jnp.transpose(drift_field, (0, 2, 1)), value_field, obstacle)
+    )(pltpu.with_memory_space_constraint(jnp.transpose(drift_field, (0, 2, 1)), pltpu.MemorySpace.HBM), value_field, obstacle)
 
 
 def solution(mesh):

time: 53.3 us -> 52.6 us (0.987)
  local copies, waits for them, and re-layouts: 2.16 us -> 1.48 us
    unnamed x4 -> x2, local copies, waits for them, and re-layouts: 2.16 us -> 1.48 us
where the time goes in v4:
time: 52.6 us; the launch traced here: 52.5 us
  Pallas kernels  50.4 us (96%)
  local copies, waits for them, and re-layouts  1.48 us (3%)
  between operations  0.64 us (1%)
    pallas_call x1, Pallas kernels, per_device(): pl.pallas_call(functools.partial(kernel, nx, ny, bx, by), out_shape=(jax....  50.4 us
    unnamed x2, local copies, waits for them, and re-layouts  1.48 us

profile of v4, /device:TPU:1, one launch (start us, length us, event | category | flops | bytes accessed | tf_op | source)
XLA Modules:
  0.0 52.5 jit_solution(14311099119010060062)
XLA Ops:
  0.6 50.4 %safe_set_steps.1 = (f32[4,8,8,1024]{3,2,1,0:T(8,128)S(1)}, f32[4]{0:T(128)S(1)}) custom-call(f32[4,2,8]{2,1,0:T(2,128)} %bitcast.1, f32[4,8,8,1024]{3,2,1,0:T(8,128)} %value_hbm.1, f32[4,8,8,1024]{3,2,1,0:T(8,128)} %barrier_hbm.1), custom_call_target="tpu_custom_call" | custom-call | tf_op jit(solution)/shard_map/safe_set_steps/pallas_call | solution.py:498
  51.0 1.0 %copy.7 = f32[4,8,8,1024]{3,2,1,0:T(8,128)} copy(f32[4,8,8,1024]{3,2,1,0:T(8,128)S(1)} %get-tuple-element.4) | data formatting | bytes 2097152
  52.0 0.5 copy.8

commit v5 on v4

--- a/solution.py
+++ b/solution.py
@@ -48,7 +48,7 @@
 
 def kernel(nx, ny, bx, by,
            drift_hbm, value_hbm, barrier_hbm, out_hbm, steps_out,
-           vb, nat_v, nat_o, ob, part_a, part_b, table, drift, pair, sent, got, rates, times, held,
+           vb, nat_v, nat_o, ob, part_a, part_b, table, drift, pair, sent, got, rates, local_rate, times, held,
            in_sem, ob_sem, drift_sem, out_sem, halo_send, halo_recv,
            pair_send, pair_recv, max_send, max_recv):
     me_x = lax.axis_index("gx")
@@ -178,7 +178,7 @@
         for j in range(by):
             both = jnp.abs(east_ends + drift[i, 0, j] * POS) + jnp.abs(north_ends + drift[i, 1, j] * POS)
             best[j % 2] = jnp.maximum(best[j % 2], both)
-    rates[0] = jnp.max(jnp.maximum(best[0], best[1]))
+    local_rate[...] = jnp.maximum(best[0], best[1])
 
     def split_obstacle(j, carry):
         for i in range(bx):
@@ -249,10 +249,10 @@
         pltpu.make_async_copy(rows, rows, sem.at[step]).wait()
 
     def largest(step, at):
-        best = [sent[step, at]] + [got[step, n, at] for n in range(3)]
-        for n in range(3, others):
-            best[n % 4] = jnp.maximum(best[n % 4], got[step, n, at])
-        return jnp.maximum(jnp.maximum(best[0], best[1]), jnp.maximum(best[2], best[3]))
+        best = [sent[step, at]] + [got[step, n, at] for n in range(7)]
+        for n in range(7, others):
+            best[n % 8] = jnp.maximum(best[n % 8], got[step, n, at])
+        return functools.reduce(jnp.maximum, best)
 
     def speed_sides(vals):
         seam_up = pltpu.roll(vals[0], NW, 1)
@@ -336,8 +336,8 @@
 
     def share(step, top):
         inner, position = inner_terms(step), position_terms(step)
-        pair[step, 0, 0] = jnp.max(top)
-        pair[step, 0, 1] = rates[0]
+        pair[step, 0, 0] = top
+        pair[step, 0, 1] = local_rate[...]
         pair_copy(step).start()
 
         def inner_rows(planes):
@@ -358,8 +358,13 @@
         each(0, 2, y_rim_rows)
         each(2, 4, x_rim_rows)
         pair_copy(step).wait_recv()
-        sent[step, 0] = jnp.maximum(pair[step, 0, 0], pair[step, 1, 0])
-        sent[step, 1] = jnp.maximum(pair[step, 0, 1], pair[step, 1, 1])
+        sent[step, 0] = jnp.max(jnp.maximum(pair[step, 0, 0], pair[step, 1, 0]))
+
+        @pl.when(step == 0)
+        def _():
+            rates[0] = jnp.max(jnp.maximum(pair[step, 0, 1], pair[step, 1, 1]))
+
+        sent[step, 1] = rates[0]
         spread(step)
 
         each(4, by, x_rim_rows)
@@ -508,10 +513,11 @@
             block,
             pltpu.VMEM((2,) + shape[2:], jnp.float32),
             pltpu.SMEM((bx, 2, by), jnp.float32),
-            pltpu.SMEM((ITERS, 2, 8), jnp.float32),
+            pltpu.VMEM((ITERS, 2, 2, NTH, LANES), jnp.float32),
             pltpu.SMEM((ITERS, 8), jnp.float32),
             pltpu.SMEM((ITERS, ny * len(PLANE) - 1, 8), jnp.float32),
             pltpu.SMEM((1,), jnp.float32),
+            pltpu.VMEM((NTH, LANES), jnp.float32),
             pltpu.VMEM((ITERS, NTH, LANES), jnp.float32),
             pltpu.VMEM((2, NTH, LANES), jnp.float32),
             dma((bx,)), dma, dma, dma((bx,)),

time: 52.6 us -> 52.5 us (level)
  no operation moved by 1% of the time
where the time goes in v5:
time: 52.5 us; the launch traced here: 52.4 us
  Pallas kernels  50.3 us (96%)
  local copies, waits for them, and re-layouts  1.48 us (3%)
  between operations  0.64 us (1%)
    pallas_call x1, Pallas kernels, per_device(): pl.pallas_call(functools.partial(kernel, nx, ny, bx, by), out_shape=(jax....  50.3 us
    unnamed x2, local copies, waits for them, and re-layouts  1.48 us

profile of v5, /device:TPU:1, one launch (start us, length us, event | category | flops | bytes accessed | tf_op | source)
XLA Modules:
  0.0 52.4 jit_solution(11572631039352410854)
XLA Ops:
  0.6 50.3 %safe_set_steps.1 = (f32[4,8,8,1024]{3,2,1,0:T(8,128)S(1)}, f32[4]{0:T(128)S(1)}) custom-call(f32[4,2,8]{2,1,0:T(2,128)} %bitcast.1, f32[4,8,8,1024]{3,2,1,0:T(8,128)} %value_hbm.1, f32[4,8,8,1024]{3,2,1,0:T(8,128)} %barrier_hbm.1), custom_call_target="tpu_custom_call" | custom-call | tf_op jit(solution)/shard_map/safe_set_steps/pallas_call | solution.py:503
  50.9 1.0 %copy.7 = f32[4,8,8,1024]{3,2,1,0:T(8,128)} copy(f32[4,8,8,1024]{3,2,1,0:T(8,128)S(1)} %get-tuple-element.4) | data formatting | bytes 2097152
  51.9 0.5 copy.8

commit v6 on v5

--- a/solution.py
+++ b/solution.py
@@ -433,7 +433,7 @@
         weight_a, weight_b = weights(step)
 
         def update(n, tops):
-            for i, j in [(i, 2 * n + m) for m in (1, 2) for i in range(1, bx + 1)]:
+            for i, j in [(i, 4 * n + m) for m in (1, 2, 3, 4) for i in range(1, bx + 1)]:
                 vals = []
                 for g in range(GROUPS):
                     s = lanes_of(g)
@@ -444,7 +444,7 @@
                 tops = row_slope(vals, tops)
             return tops
 
-        tops = lax.fori_loop(0, by // 2, update, (zero,) * 4)
+        tops = lax.fori_loop(0, by // 4, update, (zero,) * 4)
         return seam_slope(step + 1, tops)
 
     top = lax.fori_loop(0, ITERS - 1, one_step, top)

time: 52.5 us -> 52.5 us (level)
  no operation moved by 1% of the time
where the time goes in v6:
time: 52.5 us; the launch traced here: 52.4 us
  Pallas kernels  50.3 us (96%)
  local copies, waits for them, and re-layouts  1.48 us (3%)
  between operations  0.64 us (1%)
    pallas_call x1, Pallas kernels, per_device(): pl.pallas_call(functools.partial(kernel, nx, ny, bx, by), out_shape=(jax....  50.3 us
    unnamed x2, local copies, waits for them, and re-layouts  1.48 us

profile of v6, /device:TPU:1, one launch (start us, length us, event | category | flops | bytes accessed | tf_op | source)
XLA Modules:
  0.0 52.4 jit_solution(17828305942422629250)
XLA Ops:
  0.6 50.3 %safe_set_steps.1 = (f32[4,8,8,1024]{3,2,1,0:T(8,128)S(1)}, f32[4]{0:T(128)S(1)}) custom-call(f32[4,2,8]{2,1,0:T(2,128)} %bitcast.1, f32[4,8,8,1024]{3,2,1,0:T(8,128)} %value_hbm.1, f32[4,8,8,1024]{3,2,1,0:T(8,128)} %barrier_hbm.1), custom_call_target="tpu_custom_call" | custom-call | tf_op jit(solution)/shard_map/safe_set_steps/pallas_call | solution.py:503
  51.0 1.0 %copy.7 = f32[4,8,8,1024]{3,2,1,0:T(8,128)} copy(f32[4,8,8,1024]{3,2,1,0:T(8,128)S(1)} %get-tuple-element.4) | data formatting | bytes 2097152
  51.9 0.5 copy.8
